TPU v7x, 256 devices: a whole 4x4x8 slice. The times are simulated.
256 devices in a mesh: ctx: 32 (over y, x, z_hi), head: 8 (over z_lo, core).
Axes of the slice: x: 4, y: 4, z: 8 (z_hi: 2, z_lo: 4; z = z_hi * 4 + z_lo), core: 2. Of those that a mesh axis runs over, the one named last changes fastest.
Arguments:
- queries: bfloat16 [32768, 2048], P(('ctx', 'head')), may hold values from -5.5 to 5.5
- key_vecs: bfloat16 [32768, 2048], P(('ctx', 'head')), may hold values from -5.5 to 5.5
- value_vecs: bfloat16 [32768, 2048], P(('ctx', 'head')), may hold values from -6 to 6
- out_grads: bfloat16 [32768, 2048], P(('ctx', 'head')), may hold values from -6 to 6
- local_offsets: int32 [256, 4], P('ctx'), may hold values from 0 to 7, as said below
- partner_pool: int32 [32, 2, 5], replicated, may hold values from 0 to 7, as said below
- partner_picks: int32 [256, 2, 4], P('ctx'), may hold values from 0 to 4, as said below
Outputs:
- query_grads: bfloat16 [32768, 2048], P(('ctx', 'head'))
- key_grads: bfloat16 [32768, 2048], P(('ctx', 'head'))
- value_grads: bfloat16 [32768, 2048], P(('ctx', 'head'))
Inputs may be any that keep to these rules, and one draw needn't show every extreme that they name: `local_offsets`: each row holds 4 distinct offsets. `partner_pool`: each row of 5 entries names distinct blocks. `partner_picks`: each row of 4 entries holds distinct positions.
All inputs are finite; a program needn't handle non-finite values.
Results may differ from a plain program's by a relative error of at most 0.0069.
Values may be sent and summed in bfloat16 or wider, within the bound.
A program may use at most 64 MiB of HBM per device.

v0:
```python
import jax
import jax.numpy as jnp
from jax import lax
from jax.sharding import PartitionSpec as P

DH = 128
BLK = 128


def swapped(value, axis, distance):
    return lax.ppermute(value, axis, [(i, i ^ 1 << distance) for i in range(lax.axis_size(axis))])


def per_device(
    queries, key_vecs, value_vecs, out_grads, local_offsets, partner_pool, partner_picks
):
    query_heads, key_heads, value_heads, grad_heads = (
        lax.all_to_all(queries, "head", split_axis=1, concat_axis=0, tiled=True),
        lax.all_to_all(key_vecs, "head", split_axis=1, concat_axis=0, tiled=True),
        lax.all_to_all(value_vecs, "head", split_axis=1, concat_axis=0, tiled=True),
        lax.all_to_all(out_grads, "head", split_axis=1, concat_axis=0, tiled=True),
    )
    feat_width = query_heads.shape[1]
    heads_local = feat_width // DH
    blocks = query_heads.shape[0] // BLK
    bit_count = partner_pool.shape[1]
    pool_size = partner_pool.shape[2]
    group_id = lax.axis_index("ctx")
    key_blocks = key_heads.reshape(blocks, BLK, feat_width)
    value_blocks = value_heads.reshape(blocks, BLK, feat_width)
    own_pool = partner_pool[group_id]
    bit_order = list(range(bit_count))
    remote_keys = [None] * bit_count
    remote_values = [None] * bit_count
    for bit_num in bit_order:
        far_keys, far_values = swapped((key_blocks, value_blocks), "ctx", bit_num)
        remote_keys[bit_num] = far_keys[own_pool[bit_num]]
        remote_values[bit_num] = far_values[own_pool[bit_num]]
    key_table = jnp.concatenate([key_blocks] + remote_keys, axis=0)
    value_table = jnp.concatenate([value_blocks] + remote_values, axis=0)
    table_rows = key_table.shape[0]
    inner_idx = jnp.arange(blocks, dtype=jnp.int32)
    local_idx = (inner_idx[:, None] + local_offsets) % blocks
    remote_idx = (
        blocks + jnp.arange(bit_count, dtype=jnp.int32)[None, :, None] * pool_size + partner_picks
    )
    key_index = jnp.concatenate([local_idx, remote_idx.reshape(blocks, -1)], axis=1)
    key_count = key_index.shape[1]
    group_size = min(2, blocks)
    steps_total = blocks // group_size
    softmax_scale = DH ** (-0.5)
    query_blocks = query_heads.reshape(blocks, BLK, heads_local, DH)
    grad_blocks = grad_heads.reshape(blocks, BLK, heads_local, DH)

    def attend(carry_in, step_id):
        acc_key, acc_value = carry_in
        first_row = step_id * group_size
        query_part = lax.dynamic_slice_in_dim(query_blocks, first_row, group_size)
        grad_part = lax.dynamic_slice_in_dim(grad_blocks, first_row, group_size)
        chosen = lax.dynamic_slice_in_dim(key_index, first_row, group_size)
        key_part = key_table[chosen].reshape(group_size, key_count * BLK, heads_local, DH)
        value_part = value_table[chosen].reshape(group_size, key_count * BLK, heads_local, DH)
        scores = (
            jnp.einsum("gqhd,gkhd->ghqk", query_part, key_part, preferred_element_type=jnp.float32)
            * softmax_scale
        )
        row_max = jnp.max(scores, axis=-1, keepdims=True)
        exp_scores = jnp.exp(scores - row_max)
        weights = exp_scores / jnp.sum(exp_scores, axis=-1, keepdims=True)
        prob_grad = jnp.einsum(
            "gqhd,gkhd->ghqk", grad_part, value_part, preferred_element_type=jnp.float32
        )
        row_delta = jnp.sum(weights * prob_grad, axis=-1, keepdims=True)
        score_grad = (softmax_scale * weights * (prob_grad - row_delta)).astype(jnp.bfloat16)
        weights_half = weights.astype(jnp.bfloat16)
        query_out = jnp.einsum(
            "ghqk,gkhd->gqhd", score_grad, key_part, preferred_element_type=jnp.float32
        )
        key_out = jnp.einsum(
            "ghqk,gqhd->gkhd", score_grad, query_part, preferred_element_type=jnp.float32
        )
        value_out = jnp.einsum(
            "ghqk,gqhd->gkhd", weights_half, grad_part, preferred_element_type=jnp.float32
        )
        flat_index = chosen.reshape(-1)
        acc_key = acc_key.at[flat_index].add(
            key_out.reshape(group_size * key_count, BLK, feat_width)
        )
        acc_value = acc_value.at[flat_index].add(
            value_out.reshape(group_size * key_count, BLK, feat_width)
        )
        return ((acc_key, acc_value), query_out.astype(jnp.bfloat16))

    zeros_init = jnp.zeros((table_rows, BLK, feat_width), jnp.float32)
    step_ids = jnp.arange(steps_total, dtype=jnp.int32)
    (acc_key, acc_value), query_rows = lax.scan(attend, (zeros_init, zeros_init), step_ids)
    own_key = acc_key[:blocks]
    own_value = acc_value[:blocks]
    for bit_num in bit_order:
        lower = blocks + bit_num * pool_size
        sent_key = acc_key[lower : lower + pool_size]
        sent_value = acc_value[lower : lower + pool_size]
        asked_idx = partner_pool[jnp.bitwise_xor(group_id, 1 << bit_num), bit_num]
        back_key, back_value = swapped((sent_key, sent_value), "ctx", bit_num)
        own_key = own_key.at[asked_idx].add(back_key)
        own_value = own_value.at[asked_idx].add(back_value)
    query_local = query_rows.reshape(blocks * BLK, feat_width)
    key_local = own_key.reshape(blocks * BLK, feat_width).astype(jnp.bfloat16)
    value_local = own_value.reshape(blocks * BLK, feat_width).astype(jnp.bfloat16)
    query_grads, key_grads, value_grads = (
        lax.all_to_all(query_local, "head", split_axis=0, concat_axis=1, tiled=True),
        lax.all_to_all(key_local, "head", split_axis=0, concat_axis=1, tiled=True),
        lax.all_to_all(value_local, "head", split_axis=0, concat_axis=1, tiled=True),
    )
    return (query_grads, key_grads, value_grads)


def solution(mesh):
    return jax.shard_map(
        per_device,
        mesh=mesh,
        in_specs=(
            P(("ctx", "head"), None),
            P(("ctx", "head"), None),
            P(("ctx", "head"), None),
            P(("ctx", "head"), None),
            P("ctx", None),
            P(),
            P("ctx", None, None),
        ),
        out_specs=(P(("ctx", "head"), None), P(("ctx", "head"), None), P(("ctx", "head"), None)),
        check_vma=False,
    )
```

profile of v0, /device:TPU:1, one launch (start us, length us, event | category | flops | bytes accessed | tf_op | source)
XLA Modules:
  0.0 503.8 jit_solution(9401037860144758824)
XLA Ops:
  0.7 2.1 copy.64
  2.8 7.4 %all-to-all-start = ((bf16[128,8,256]{0,2,1:T(8,128)(2,1)}), bf16[128,8,256]{0,2,1:T(8,128)(2,1)S(1)}, u32[]{:S(2)}, u32[]{:S(2)}) async-start(bf16[128,8,256]{0,2,1:T(8,128)(2,1)} %bitcast.7), calls=%async_computation | async-start | bytes 1048576 | tf_op jit(solution)/shard_map/all_to_all | solution.py:18
  11.2 13.4 %all-to-all-done = bf16[128,8,256]{0,2,1:T(8,128)(2,1)S(1)} async-done(((bf16[128,8,256]{0,2,1:T(8,128)(2,1)}), bf16[128,8,256]{0,2,1:T(8,128)(2,1)S(1)}, u32[]{:S(2)}, u32[]{:S(2)}) %all-to-all-start) | async-done | bytes 524320 | tf_op jit(solution)/shard_map/all_to_all | solution.py:18
  24.5 4.4 all-to-all-start.1
  29.9 13.4 %all-to-all-done.1 = bf16[128,8,256]{0,2,1:T(8,128)(2,1)S(1)} async-done(((bf16[128,8,256]{0,2,1:T(8,128)(2,1)}), bf16[128,8,256]{0,2,1:T(8,128)(2,1)S(1)}, u32[]{:S(2)}, u32[]{:S(2)}) %all-to-all-start.1) | async-done | bytes 524320 | tf_op jit(solution)/shard_map/all_to_all | solution.py:19
  43.3 4.4 all-to-all-start.3
  49.9 12.2 %all-to-all-done.3 = bf16[128,8,256]{0,2,1:T(8,128)(2,1)S(1)} async-done(((bf16[128,8,256]{0,2,1:T(8,128)(2,1)}), bf16[128,8,256]{0,2,1:T(8,128)(2,1)S(1)}, u32[]{:S(2)}, u32[]{:S(2)}) %all-to-all-start.3) | async-done | bytes 524320 | tf_op jit(solution)/shard_map/all_to_all | solution.py:20
  62.0 5.0 all-to-all-start.2
  68.3 4.4 collective-permute-start.2
  74.0 6.4 %collective-permute-done.3 = bf16[8,128,256]{1,2,0:T(8,128)(2,1)} collective-permute-done((bf16[8,128,256]{1,2,0:T(8,128)(2,1)S(1)}, bf16[8,128,256]{1,2,0:T(8,128)(2,1)}, u32[]{:S(2)}, u32[]{:S(2)}) %collective-permute-start.3) | collective-permute-done | bytes 524320 | tf_op jit(solution)/shard_map/ppermute | solution.py:11
  82.1 32.8 %collective-permute-done.2 = bf16[8,128,256]{1,2,0:T(8,128)(2,1)S(1)} collective-permute-done((bf16[8,128,256]{1,2,0:T(8,128)(2,1)S(1)}, bf16[8,128,256]{1,2,0:T(8,128)(2,1)S(1)}, u32[]{:S(2)}, u32[]{:S(2)}) %collective-permute-start.2) | collective-permute-done | bytes 524320 | tf_op jit(solution)/shard_map/ppermute | solution.py:11
  118.8 7.4 %collective-permute-done = bf16[8,128,256]{1,2,0:T(8,128)(2,1)} collective-permute-done((bf16[8,128,256]{1,2,0:T(8,128)(2,1)S(1)}, bf16[8,128,256]{1,2,0:T(8,128)(2,1)}, u32[]{:S(2)}, u32[]{:S(2)}) %collective-permute-start) | collective-permute-done | bytes 524320 | tf_op jit(solution)/shard_map/ppermute | solution.py:11
  129.0 2.4 copy.70
  134.9 245.3 %while.14 = (s32[]{:T(128)}, f32[18,128,256]{2,1,0:T(8,128)}, f32[18,128,256]{2,1,0:T(8,128)}, bf16[4,2,128,2,128]{2,4,3,1,0:T(8,128)(2,1)}, s32[4]{0:T(128)S(1)...) while((s32[]{:T(128)}, f32[18,128,256]{2,1,0:T(8,128)}, ...), condition=%wide.region_6.7_spmd, body=%wide.region_0.6_spmd.sunk | while | flops 1018497152 | bytes 127551168 | solution.py:96
  142.6 3.7 fusion.59
  146.4 3.0 multiply_reduce_fusion.2
  151.2 3.2 convolution_bitcast_fusion.5
  154.4 5.7 %copy.96 = f32[2,1536,2,128]{3,2,1,0:T(2,128)} copy(f32[2,1536,2,128]{1,3,2,0:T(8,128)} %convolution_bitcast_fusion.5) | data formatting | bytes 6291456 | tf_op jit(solution)/shard_map/while/body/eval_jaxpr/ghqk,gqhd->gkhd/transpose | solution.py:82
  160.2 5.5 %reshape.353 = f32[24,128,256]{2,1,0:T(8,128)} reshape(f32[2,1536,2,128]{3,2,1,0:T(2,128)} %copy.96) | data formatting | bytes 6291456 | tf_op jit(solution)/shard_map/while/body/eval_jaxpr/reshape | solution.py:90
  165.7 9.8 %scatter_fusion.1 = f32[18,128,256]{2,1,0:T(8,128)} fusion(f32[18,128,256]{2,1,0:T(8,128)} %get-tuple-element.228, s32[24]{0:T(128)S(1)} %fusion.58, f32[24,128,256]{2,1,0:T(8,128)} %reshape.353), kind=kCustom, calls=%fused_computation.7.clone.1 | custom fusion | flops 786432 | bytes 9437280 | tf_op jit(solution)/shard_map/while/body/eval_jaxpr/scatter-add | solution.py:89
  175.5 3.1 convolution_bitcast_fusion.4
  178.6 4.2 copy.95
  182.8 3.7 reshape.352
  186.5 9.8 %scatter_fusion = f32[18,128,256]{2,1,0:T(8,128)} fusion(f32[18,128,256]{2,1,0:T(8,128)} %get-tuple-element.227, s32[24]{0:T(128)S(1)} %fusion.58, f32[24,128,256]{2,1,0:T(8,128)} %reshape.352), kind=kCustom, calls=%fused_computation.6.clone.1 | custom fusion | flops 786432 | bytes 9437280 | tf_op jit(solution)/shard_map/while/body/eval_jaxpr/scatter-add | solution.py:86
  204.0 3.7 fusion.59
  207.7 3.0 multiply_reduce_fusion.2
  212.6 3.2 convolution_bitcast_fusion.5
  215.8 5.7 %copy.96 = f32[2,1536,2,128]{3,2,1,0:T(2,128)} copy(f32[2,1536,2,128]{1,3,2,0:T(8,128)} %convolution_bitcast_fusion.5) | data formatting | bytes 6291456 | tf_op jit(solution)/shard_map/while/body/eval_jaxpr/ghqk,gqhd->gkhd/transpose | solution.py:82
  221.5 5.5 %reshape.353 = f32[24,128,256]{2,1,0:T(8,128)} reshape(f32[2,1536,2,128]{3,2,1,0:T(2,128)} %copy.96) | data formatting | bytes 6291456 | tf_op jit(solution)/shard_map/while/body/eval_jaxpr/reshape | solution.py:90
  227.0 9.8 %scatter_fusion.1 = f32[18,128,256]{2,1,0:T(8,128)} fusion(f32[18,128,256]{2,1,0:T(8,128)} %get-tuple-element.228, s32[24]{0:T(128)S(1)} %fusion.58, f32[24,128,256]{2,1,0:T(8,128)} %reshape.353), kind=kCustom, calls=%fused_computation.7.clone.1 | custom fusion | flops 786432 | bytes 9437280 | tf_op jit(solution)/shard_map/while/body/eval_jaxpr/scatter-add | solution.py:89
  236.8 3.1 convolution_bitcast_fusion.4
  239.9 4.2 copy.95
  244.1 3.7 reshape.352
  247.8 9.8 %scatter_fusion = f32[18,128,256]{2,1,0:T(8,128)} fusion(f32[18,128,256]{2,1,0:T(8,128)} %get-tuple-element.227, s32[24]{0:T(128)S(1)} %fusion.58, f32[24,128,256]{2,1,0:T(8,128)} %reshape.352), kind=kCustom, calls=%fused_computation.6.clone.1 | custom fusion | flops 786432 | bytes 9437280 | tf_op jit(solution)/shard_map/while/body/eval_jaxpr/scatter-add | solution.py:86
  265.3 3.7 fusion.59
  269.1 3.0 multiply_reduce_fusion.2
  273.9 3.2 convolution_bitcast_fusion.5
  277.1 5.7 %copy.96 = f32[2,1536,2,128]{3,2,1,0:T(2,128)} copy(f32[2,1536,2,128]{1,3,2,0:T(8,128)} %convolution_bitcast_fusion.5) | data formatting | bytes 6291456 | tf_op jit(solution)/shard_map/while/body/eval_jaxpr/ghqk,gqhd->gkhd/transpose | solution.py:82
  282.9 5.5 %reshape.353 = f32[24,128,256]{2,1,0:T(8,128)} reshape(f32[2,1536,2,128]{3,2,1,0:T(2,128)} %copy.96) | data formatting | bytes 6291456 | tf_op jit(solution)/shard_map/while/body/eval_jaxpr/reshape | solution.py:90
  288.4 9.7 %scatter_fusion.1 = f32[18,128,256]{2,1,0:T(8,128)} fusion(f32[18,128,256]{2,1,0:T(8,128)} %get-tuple-element.228, s32[24]{0:T(128)S(1)} %fusion.58, f32[24,128,256]{2,1,0:T(8,128)} %reshape.353), kind=kCustom, calls=%fused_computation.7.clone.1 | custom fusion | flops 786432 | bytes 9437280 | tf_op jit(solution)/shard_map/while/body/eval_jaxpr/scatter-add | solution.py:89
  298.0 3.1 convolution_bitcast_fusion.4
  301.1 4.2 copy.95
  305.3 3.7 reshape.352
  309.0 9.7 %scatter_fusion = f32[18,128,256]{2,1,0:T(8,128)} fusion(f32[18,128,256]{2,1,0:T(8,128)} %get-tuple-element.227, s32[24]{0:T(128)S(1)} %fusion.58, f32[24,128,256]{2,1,0:T(8,128)} %reshape.352), kind=kCustom, calls=%fused_computation.6.clone.1 | custom fusion | flops 786432 | bytes 9437280 | tf_op jit(solution)/shard_map/while/body/eval_jaxpr/scatter-add | solution.py:86
  326.5 3.7 fusion.59
  330.2 3.0 multiply_reduce_fusion.2
  335.1 3.2 convolution_bitcast_fusion.5
  338.3 5.7 %copy.96 = f32[2,1536,2,128]{3,2,1,0:T(2,128)} copy(f32[2,1536,2,128]{1,3,2,0:T(8,128)} %convolution_bitcast_fusion.5) | data formatting | bytes 6291456 | tf_op jit(solution)/shard_map/while/body/eval_jaxpr/ghqk,gqhd->gkhd/transpose | solution.py:82
  344.0 5.5 %reshape.353 = f32[24,128,256]{2,1,0:T(8,128)} reshape(f32[2,1536,2,128]{3,2,1,0:T(2,128)} %copy.96) | data formatting | bytes 6291456 | tf_op jit(solution)/shard_map/while/body/eval_jaxpr/reshape | solution.py:90
  349.5 9.8 %scatter_fusion.1 = f32[18,128,256]{2,1,0:T(8,128)} fusion(f32[18,128,256]{2,1,0:T(8,128)} %get-tuple-element.228, s32[24]{0:T(128)S(1)} %fusion.58, f32[24,128,256]{2,1,0:T(8,128)} %reshape.353), kind=kCustom, calls=%fused_computation.7.clone.1 | custom fusion | flops 786432 | bytes 9437280 | tf_op jit(solution)/shard_map/while/body/eval_jaxpr/scatter-add | solution.py:89
  359.4 3.1 convolution_bitcast_fusion.4
  362.5 4.2 copy.95
  366.7 3.7 reshape.352
  370.3 9.8 %scatter_fusion = f32[18,128,256]{2,1,0:T(8,128)} fusion(f32[18,128,256]{2,1,0:T(8,128)} %get-tuple-element.227, s32[24]{0:T(128)S(1)} %fusion.58, f32[24,128,256]{2,1,0:T(8,128)} %reshape.352), kind=kCustom, calls=%fused_computation.6.clone.1 | custom fusion | flops 786432 | bytes 9437280 | tf_op jit(solution)/shard_map/while/body/eval_jaxpr/scatter-add | solution.py:86
  382.2 5.4 %all-to-all-start.4 = ((bf16[8,128,256]{2,1,0:T(8,128)(2,1)}), bf16[8,128,256]{2,1,0:T(8,128)(2,1)}, u32[]{:S(2)}, u32[]{:S(2)}) async-start(bf16[8,128,256]{2,1,0:T(8,128)(2,1)} %copy.80), calls=%async_computation.4 | async-start | bytes 1048576 | tf_op jit(solution)/shard_map/all_to_all | solution.py:111
  387.6 2.2 fusion.34
  393.4 33.4 %collective-permute-done.4 = f32[5,128,256]{2,1,0:T(8,128)S(1)} collective-permute-done((f32[5,128,256]{2,1,0:T(8,128)S(1)}, f32[5,128,256]{2,1,0:T(8,128)S(1)}, u32[]{:S(2)}, u32[]{:S(2)}) %collective-permute-start.4) | collective-permute-done | bytes 655392 | tf_op jit(solution)/shard_map/ppermute | solution.py:11
  428.0 2.2 scatter_fusion.3
  431.1 5.4 %all-to-all-start.5 = ((bf16[8,128,256]{2,1,0:T(8,128)(2,1)}), bf16[8,128,256]{2,1,0:T(8,128)(2,1)}, u32[]{:S(2)}, u32[]{:S(2)}) async-start(bf16[8,128,256]{2,1,0:T(8,128)(2,1)} %convert_element_type.20), calls=%async_computation.5 | async-start | bytes 1048576 | tf_op jit(solution)/shard_map/all_to_all | solution.py:112
  437.5 3.9 collective-permute-start.6
  442.9 35.3 %collective-permute-done.6 = f32[5,128,256]{2,1,0:T(8,128)} collective-permute-done((f32[5,128,256]{2,1,0:T(8,128)S(1)}, f32[5,128,256]{2,1,0:T(8,128)}, u32[]{:S(2)}, u32[]{:S(2)}) %collective-permute-start.6) | collective-permute-done | bytes 655392 | tf_op jit(solution)/shard_map/ppermute | solution.py:11
  480.4 2.1 scatter_fusion.5
  483.3 5.3 %all-to-all-start.6 = ((bf16[8,128,256]{2,1,0:T(8,128)(2,1)}), bf16[8,128,256]{2,1,0:T(8,128)(2,1)S(1)}, u32[]{:S(2)}, u32[]{:S(2)}) async-start(bf16[8,128,256]{2,1,0:T(8,128)(2,1)} %convert_element_type.21), calls=%async_computation.6 | async-start | bytes 1048576 | tf_op jit(solution)/shard_map/all_to_all | solution.py:113
  492.8 10.1 %all-to-all-done.6 = bf16[8,128,256]{2,1,0:T(8,128)(2,1)S(1)} async-done(((bf16[8,128,256]{2,1,0:T(8,128)(2,1)}), bf16[8,128,256]{2,1,0:T(8,128)(2,1)S(1)}, u32[]{:S(2)}, u32[]{:S(2)}) %all-to-all-start.6) | async-done | bytes 524320 | tf_op jit(solution)/shard_map/all_to_all | solution.py:113
  (167 shorter events, 72.1 us)
Async XLA Ops:
  0.6 9.5 %copy-start.7 = (bf16[128,2048]{1,0:T(8,128)(2,1)S(1)}, bf16[128,2048]{1,0:T(8,128)(2,1)}, u32[]{:S(2)}) copy-start(bf16[128,2048]{1,0:T(8,128)(2,1)} %param.10) | copy-start | bytes 1572868
  0.6 28.3 %copy-start.8 = (bf16[128,2048]{1,0:T(8,128)(2,1)S(1)}, bf16[128,2048]{1,0:T(8,128)(2,1)}, u32[]{:S(2)}) copy-start(bf16[128,2048]{1,0:T(8,128)(2,1)} %param.11) | copy-start | bytes 1572868
  2.8 21.8 %all-to-all-start = ((bf16[128,8,256]{0,2,1:T(8,128)(2,1)}), bf16[128,8,256]{0,2,1:T(8,128)(2,1)S(1)}, u32[]{:S(2)}, u32[]{:S(2)}) async-start(bf16[128,8,256]{0,2,1:T(8,128)(2,1)} %bitcast.7), calls=%async_computation | async-start | bytes 1048576 | tf_op jit(solution)/shard_map/all_to_all | solution.py:18
  10.2 37.5 %copy-start.9 = (bf16[128,2048]{1,0:T(8,128)(2,1)S(1)}, bf16[128,2048]{1,0:T(8,128)(2,1)}, u32[]{:S(2)}) copy-start(bf16[128,2048]{1,0:T(8,128)(2,1)} %param.12) | copy-start | bytes 1572868
  11.2 37.5 %copy-start.10 = (s32[32,2,5]{0,1,2:T(2,128)S(1)}, s32[32,2,5]{0,1,2:T(2,128)}, u32[]{:S(2)}) copy-start(s32[32,2,5]{0,1,2:T(2,128)} %param.14) | copy-start | bytes 3844
  11.2 38.6 %copy-start.12 = (s32[8,4]{0,1:T(4,128)S(1)}, s32[8,4]{0,1:T(4,128)}, u32[]{:S(2)}) copy-start(s32[8,4]{0,1:T(4,128)} %param.13) | copy-start | bytes 388
  11.2 38.6 %copy-start.11 = (s32[8,2,4]{0,2,1:T(4,128)S(1)}, s32[8,2,4]{0,2,1:T(4,128)}, u32[]{:S(2)}) copy-start(s32[8,2,4]{0,2,1:T(4,128)} %param.15) | copy-start | bytes 772
  24.5 18.8 %all-to-all-start.1 = ((bf16[128,8,256]{0,2,1:T(8,128)(2,1)}), bf16[128,8,256]{0,2,1:T(8,128)(2,1)S(1)}, u32[]{:S(2)}, u32[]{:S(2)}) async-start(bf16[128,8,256]{0,2,1:T(8,128)(2,1)} %bitcast.10), calls=%async_computation.1 | async-start | bytes 1048576 | tf_op jit(solution)/shard_map/all_to_all | solution.py:19
  43.3 18.8 %all-to-all-start.3 = ((bf16[128,8,256]{0,2,1:T(8,128)(2,1)}), bf16[128,8,256]{0,2,1:T(8,128)(2,1)S(1)}, u32[]{:S(2)}, u32[]{:S(2)}) async-start(bf16[128,8,256]{0,2,1:T(8,128)(2,1)} %bitcast.17), calls=%async_computation.3 | async-start | bytes 1048576 | tf_op jit(solution)/shard_map/all_to_all | solution.py:20
  62.0 69.4 %all-to-all-start.2 = ((bf16[128,8,256]{0,2,1:T(8,128)(2,1)}), bf16[128,8,256]{0,2,1:T(8,128)(2,1)}, u32[]{:S(2)}, u32[]{:S(2)}) async-start(bf16[128,8,256]{0,2,1:T(8,128)(2,1)} %bitcast.14), calls=%async_computation.2 | async-start | bytes 1048576 | tf_op jit(solution)/shard_map/all_to_all | solution.py:21
  67.0 13.4 %collective-permute-start.3 = (bf16[8,128,256]{1,2,0:T(8,128)(2,1)S(1)}, bf16[8,128,256]{1,2,0:T(8,128)(2,1)}, u32[]{:S(2)}, u32[]{:S(2)}) collective-permute-start(bf16[8,128,256]{1,2,0:T(8,128)(2,1)S(1)} %bitcast.80), channel_id=1, source_target_pairs={{0,16},{8,24},{16,0},{24,8},{32,48},{40,56},{48,32},{56,40},{64,80... | collective-permute-start | bytes 1572872 | tf_op jit(solution)/shard_map/ppermute | solution.py:11
  68.3 46.6 %collective-permute-start.2 = (bf16[8,128,256]{1,2,0:T(8,128)(2,1)S(1)}, bf16[8,128,256]{1,2,0:T(8,128)(2,1)S(1)}, u32[]{:S(2)}, u32[]{:S(2)}) collective-permute-start(bf16[8,128,256]{1,2,0:T(8,128)(2,1)S(1)} %bitcast.81), channel_id=1, source_target_pairs={{0,8},{8,0},{16,24},{24,16},{32,40},{40,32},{48,56},{56,48},{64,72... | collective-permute-start | bytes 1572872 | tf_op jit(solution)/shard_map/ppermute | solution.py:11
  72.7 45.5 %collective-permute-start.1 = (bf16[8,128,256]{1,2,0:T(8,128)(2,1)S(1)}, bf16[8,128,256]{1,2,0:T(8,128)(2,1)S(1)}, u32[]{:S(2)}, u32[]{:S(2)}) collective-permute-start(bf16[8,128,256]{1,2,0:T(8,128)(2,1)S(1)} %bitcast.77), channel_id=1, source_target_pairs={{0,16},{8,24},{16,0},{24,8},{32,48},{40,56},{48,32},{56,40},{64,80... | collective-permute-start | bytes 1572872 | tf_op jit(solution)/shard_map/ppermute | solution.py:11
  72.9 53.3 %collective-permute-start = (bf16[8,128,256]{1,2,0:T(8,128)(2,1)S(1)}, bf16[8,128,256]{1,2,0:T(8,128)(2,1)}, u32[]{:S(2)}, u32[]{:S(2)}) collective-permute-start(bf16[8,128,256]{1,2,0:T(8,128)(2,1)S(1)} %bitcast.78), channel_id=1, source_target_pairs={{0,8},{8,0},{16,24},{24,16},{32,40},{40,32},{48,56},{56,48},{64,72... | collective-permute-start | bytes 1572872 | tf_op jit(solution)/shard_map/ppermute | solution.py:11
  134.9 1.6 copy-start.5
  134.9 4.2 copy-start.2
  142.6 3.8 copy-start.4
  146.4 3.0 copy-start
  186.5 9.8 %copy-start.3 = (bf16[18,128,256]{2,1,0:T(8,128)(2,1)S(1)}, bf16[18,128,256]{2,1,0:T(8,128)(2,1)}, u32[]{:S(2)}) copy-start(bf16[18,128,256]{2,1,0:T(8,128)(2,1)} %copy-done.2) | copy-start | bytes 3538948 | tf_op jit(solution)/shard_map/while
  186.5 9.8 %copy-start.6 = (bf16[8,128,2,128]{1,3,2,0:T(8,128)(2,1)S(1)}, bf16[8,128,2,128]{1,3,2,0:T(8,128)(2,1)}, u32[]{:S(2)}) copy-start(bf16[8,128,2,128]{1,3,2,0:T(8,128)(2,1)} %copy-done.5) | copy-start | bytes 1572868 | tf_op jit(solution)/shard_map/while
  196.2 1.6 copy-start.5
  196.2 4.2 copy-start.2
  204.0 3.8 copy-start.4
  207.7 3.0 copy-start
  247.8 9.8 %copy-start.3 = (bf16[18,128,256]{2,1,0:T(8,128)(2,1)S(1)}, bf16[18,128,256]{2,1,0:T(8,128)(2,1)}, u32[]{:S(2)}) copy-start(bf16[18,128,256]{2,1,0:T(8,128)(2,1)} %copy-done.2) | copy-start | bytes 3538948 | tf_op jit(solution)/shard_map/while
  247.8 9.8 %copy-start.6 = (bf16[8,128,2,128]{1,3,2,0:T(8,128)(2,1)S(1)}, bf16[8,128,2,128]{1,3,2,0:T(8,128)(2,1)}, u32[]{:S(2)}) copy-start(bf16[8,128,2,128]{1,3,2,0:T(8,128)(2,1)} %copy-done.5) | copy-start | bytes 1572868 | tf_op jit(solution)/shard_map/while
  257.6 1.6 copy-start.5
  257.6 4.2 copy-start.2
  265.3 3.8 copy-start.4
  269.1 3.0 copy-start
  309.0 9.7 %copy-start.3 = (bf16[18,128,256]{2,1,0:T(8,128)(2,1)S(1)}, bf16[18,128,256]{2,1,0:T(8,128)(2,1)}, u32[]{:S(2)}) copy-start(bf16[18,128,256]{2,1,0:T(8,128)(2,1)} %copy-done.2) | copy-start | bytes 3538948 | tf_op jit(solution)/shard_map/while
  309.0 9.7 %copy-start.6 = (bf16[8,128,2,128]{1,3,2,0:T(8,128)(2,1)S(1)}, bf16[8,128,2,128]{1,3,2,0:T(8,128)(2,1)}, u32[]{:S(2)}) copy-start(bf16[8,128,2,128]{1,3,2,0:T(8,128)(2,1)} %copy-done.5) | copy-start | bytes 1572868 | tf_op jit(solution)/shard_map/while
  318.7 1.6 copy-start.5
  318.7 4.2 copy-start.2
  326.5 3.8 copy-start.4
  330.2 3.0 copy-start
  370.3 9.8 %copy-start.3 = (bf16[18,128,256]{2,1,0:T(8,128)(2,1)S(1)}, bf16[18,128,256]{2,1,0:T(8,128)(2,1)}, u32[]{:S(2)}) copy-start(bf16[18,128,256]{2,1,0:T(8,128)(2,1)} %copy-done.2) | copy-start | bytes 3538948 | tf_op jit(solution)/shard_map/while
  370.3 9.8 %copy-start.6 = (bf16[8,128,2,128]{1,3,2,0:T(8,128)(2,1)S(1)}, bf16[8,128,2,128]{1,3,2,0:T(8,128)(2,1)}, u32[]{:S(2)}) copy-start(bf16[8,128,2,128]{1,3,2,0:T(8,128)(2,1)} %copy-done.5) | copy-start | bytes 1572868 | tf_op jit(solution)/shard_map/while
  380.2 11.9 %copy-start.13 = (s32[5]{0:T(128)S(1)}, s32[5]{0:T(128)}, u32[]{:S(2)}) copy-start(s32[5]{0:T(128)} %get-tuple-element.103) | copy-start | bytes 64
  380.2 11.9 %copy-start.14 = (s32[5]{0:T(128)S(1)}, s32[5]{0:T(128)}, u32[]{:S(2)}) copy-start(s32[5]{0:T(128)} %get-tuple-element.106) | copy-start | bytes 64
  382.2 48.8 %all-to-all-start.4 = ((bf16[8,128,256]{2,1,0:T(8,128)(2,1)}), bf16[8,128,256]{2,1,0:T(8,128)(2,1)}, u32[]{:S(2)}, u32[]{:S(2)}) async-start(bf16[8,128,256]{2,1,0:T(8,128)(2,1)} %copy.80), calls=%async_computation.4 | async-start | bytes 1048576 | tf_op jit(solution)/shard_map/all_to_all | solution.py:111
  389.8 37.0 %collective-permute-start.4 = (f32[5,128,256]{2,1,0:T(8,128)S(1)}, f32[5,128,256]{2,1,0:T(8,128)S(1)}, u32[]{:S(2)}, u32[]{:S(2)}) collective-permute-start(f32[5,128,256]{2,1,0:T(8,128)S(1)} %get-tuple-element.136), channel_id=1, source_target_pairs={{0,8},{8,0},{16,24},{24,16},{32,40},{40,32},{48,56},{56,48},{64,72... | collective-permute-start | bytes 1966088 | tf_op jit(solution)/shard_map/ppermute | solution.py:11
  391.3 36.7 %collective-permute-start.5 = (f32[5,128,256]{2,1,0:T(8,128)}, f32[5,128,256]{2,1,0:T(8,128)}, u32[]{:S(2)}, u32[]{:S(2)}) collective-permute-start(f32[5,128,256]{2,1,0:T(8,128)} %get-tuple-element.135), channel_id=1, source_target_pairs={{0,16},{8,24},{16,0},{24,8},{32,48},{40,56},{48,32},{56,40},{64,80... | collective-permute-start | bytes 1966088 | tf_op jit(solution)/shard_map/ppermute | solution.py:11
  428.0 8.5 %copy-start.1 = (f32[18,128,256]{2,1,0:T(8,128)S(1)}, f32[18,128,256]{2,1,0:T(8,128)}, u32[]{:S(2)}) copy-start(f32[18,128,256]{2,1,0:T(8,128)} %get-tuple-element.59) | copy-start | bytes 7077892
  431.1 52.2 %all-to-all-start.5 = ((bf16[8,128,256]{2,1,0:T(8,128)(2,1)}), bf16[8,128,256]{2,1,0:T(8,128)(2,1)}, u32[]{:S(2)}, u32[]{:S(2)}) async-start(bf16[8,128,256]{2,1,0:T(8,128)(2,1)} %convert_element_type.20), calls=%async_computation.5 | async-start | bytes 1048576 | tf_op jit(solution)/shard_map/all_to_all | solution.py:112
  437.5 40.8 %collective-permute-start.6 = (f32[5,128,256]{2,1,0:T(8,128)S(1)}, f32[5,128,256]{2,1,0:T(8,128)}, u32[]{:S(2)}, u32[]{:S(2)}) collective-permute-start(f32[5,128,256]{2,1,0:T(8,128)S(1)} %get-tuple-element.134), channel_id=1, source_target_pairs={{0,8},{8,0},{16,24},{24,16},{32,40},{40,32},{48,56},{56,48},{64,72... | collective-permute-start | bytes 1966088 | tf_op jit(solution)/shard_map/ppermute | solution.py:11
  441.4 39.0 %collective-permute-start.7 = (f32[5,128,256]{2,1,0:T(8,128)}, f32[5,128,256]{2,1,0:T(8,128)}, u32[]{:S(2)}, u32[]{:S(2)}) collective-permute-start(f32[5,128,256]{2,1,0:T(8,128)} %get-tuple-element.133), channel_id=1, source_target_pairs={{0,16},{8,24},{16,0},{24,8},{32,48},{40,56},{48,32},{56,40},{64,80... | collective-permute-start | bytes 1966088 | tf_op jit(solution)/shard_map/ppermute | solution.py:11
  483.3 19.7 %all-to-all-start.6 = ((bf16[8,128,256]{2,1,0:T(8,128)(2,1)}), bf16[8,128,256]{2,1,0:T(8,128)(2,1)S(1)}, u32[]{:S(2)}, u32[]{:S(2)}) async-start(bf16[8,128,256]{2,1,0:T(8,128)(2,1)} %convert_element_type.21), calls=%async_computation.6 | async-start | bytes 1048576 | tf_op jit(solution)/shard_map/all_to_all | solution.py:113
where the time goes:
time: 507 us; the launch traced here: 504 us
  waiting for transfers between devices  164 us (32%)
  local copies, waits for them, and re-layouts  134 us (26%)
  other arithmetic  92.3 us (18%)
  matrix products  57.2 us (11%)
  starting transfers between devices  51.7 us (10%)
    ppermute x8, waiting for transfers between devices, swapped(): lax.ppermute(value, axis, [(i, i ^ 1 << distance) for i in range(lax.axis...  115 us
    scatter-add x4, other arithmetic, attend(): acc_value.at[flat_index]  39.1 us
    scatter-add x4, other arithmetic, attend(): acc_key.at[flat_index]  39.1 us
    transpose x4, local copies, waits for them, and re-layouts, attend(): jnp.einsum('ghqk,gqhd->gkhd', weights_half, grad_part, preferred_element_...  22.9 us
    reshape x4, local copies, waits for them, and re-layouts, attend(): value_out.reshape(group_size * key_count, BLK, feat_width)  22.1 us
    transpose x4, local copies, waits for them, and re-layouts, attend(): jnp.einsum('ghqk,gqhd->gkhd', score_grad, query_part, preferred_element_t...  16.7 us
    sub x4, matrix products, attend(): exp_scores = jnp.exp(scores - row_max)  15 us
    reshape x4, local copies, waits for them, and re-layouts, attend(): key_out.reshape(group_size * key_count, BLK, feat_width)  14.7 us
  transfers between devices with their start and end apart: 15, of which 9 were waited for; matrix products, arithmetic and copies ran while one was open for 7% of the time, Pallas kernels for 0%

commit v1 on v0

v1 whole, which is shorter than its diff:
```python
import jax
import jax.numpy as jnp
from jax import lax
from jax.experimental import pallas as pl
from jax.experimental.pallas import tpu as pltpu
from jax.sharding import PartitionSpec as P

MESH = pl.DeviceIdType.MESH
DH = 128
BLK = 128
NKEY = 12
TILES = 18
ZERO = 16 * NKEY
SCALE = DH**-0.5
f32 = jnp.float32
bf16 = jnp.bfloat16
ORDER = [(dx, dz) for dz in (4, 3, 5, 2, 6, 1, 7, 0) for dx in (1, 0)]


def place():
    ctx = lax.axis_index("ctx")
    head = lax.axis_index("head")
    return ctx, (ctx // 2) % 2, (ctx % 2) * 4 + head // 2, head % 2


def device(ctx, xb, z, core):
    return ((ctx // 4) * 4 + xb * 2 + z // 4, (z % 4) * 2 + core)


def greet(ctx, targets, count):
    barrier = pltpu.get_barrier_semaphore()
    for cond, (xb, z, core) in targets:

        @pl.when(cond)
        def _(xb=xb, z=z, core=core):
            pl.semaphore_signal(
                barrier, 1, device_id=device(ctx, xb, z, core), device_id_type=MESH
            )

    pl.semaphore_wait(barrier, count)


def remote(src, dst, ssem, rsem, dev):
    return pltpu.make_async_remote_copy(
        src_ref=src, dst_ref=dst, send_sem=ssem, recv_sem=rsem, device_id=dev, device_id_type=MESH
    )


def scatter_kernel(q, k, v, g, meta, qd, kv, rmeta, ssem, rsem, fsem, msem):
    ctx, xb, z, core = place()
    qd[:, 0:128, 128:256] = jnp.zeros((16, 128, 128), bf16)
    qd[:, 128:256, 0:128] = jnp.zeros((16, 128, 128), bf16)
    away = core != xb
    others = []
    for s in range(8):
        zs = (z + s) % 8
        for c in range(2):
            cond = jnp.logical_or(away, jnp.logical_or(zs != z, core != c))
            others.append((cond, (core, zs, c)))
    others.append((away, (xb, z, 1 - core)))
    greet(ctx, others, 16)
    slot = z * 2 + core

    def dst(a):
        if a == 0:
            return kv.at[slot, :, 0:128]
        if a == 1:
            return kv.at[slot, :, 128:256]
        if a == 2:
            return qd.at[slot, 0:128, 0:128]
        return qd.at[slot, 128:256, 128:256]

    srcs = (k, v, q, g)
    for a0 in (0, 2):
        for o, (dx, dz) in enumerate(ORDER):
            xd, zd = xb ^ dx, (z + dz) % 8
            cols = pl.ds(pl.multiple_of((xd * 8 + zd) * 128, 128), 128)
            for a in (a0, a0 + 1):
                src = srcs[a].at[:, cols]
                rc = remote(src, dst(a), ssem.at[a, o], rsem.at[a, slot], device(ctx, xd, zd, xb))
                if (dx, dz) == (0, 0):

                    @pl.when(away)
                    def _(rc=rc):
                        rc.start()

                    @pl.when(jnp.logical_not(away))
                    def _(src=src, a=a):
                        pltpu.make_async_copy(src, dst(a), rsem.at[a, slot]).start()
                else:
                    rc.start()
    mine = (z % 4) * 2 + core
    mrow = z // 4
    for dx in (0, 1):
        rc = remote(
            meta, rmeta.at[mrow], msem.at[0, dx], msem.at[1, mrow], device(ctx, xb ^ dx, mine, xb)
        )
        if dx == 1:
            rc.start()
        else:
            here = jnp.logical_and(jnp.logical_not(away), mine == z)

            @pl.when(jnp.logical_not(here))
            def _(rc=rc):
                rc.start()

            @pl.when(here)
            def _():
                pltpu.make_async_copy(meta, rmeta.at[mrow], msem.at[1, mrow]).start()

    here_dev = device(ctx, xb, z, 1 - core)

    def arrived(a, n, ref):
        remote(ref, ref, ssem.at[a, 0], rsem.at[a, n], here_dev).wait_recv()

    for n in range(16):
        arrived(0, n, kv.at[n, :, 0:128])
        arrived(1, n, kv.at[n, :, 128:256])
    forward = remote(kv.at[0:16], kv.at[16:32], fsem.at[0], fsem.at[1], here_dev)
    forward.start()
    for n in range(16):
        arrived(2, n, qd.at[n, 0:128, 0:128])
        arrived(3, n, qd.at[n, 128:256, 128:256])
    forward.wait()
    for n in range(2):
        remote(meta, rmeta.at[n], msem.at[0, 0], msem.at[1, n], here_dev).wait_recv()
    for o, (dx, dz) in enumerate(ORDER):
        for a in range(4):
            src = srcs[a].at[:, 0:128]
            rc = remote(src, src, ssem.at[a, o], rsem.at[a, 0], here_dev)
            if (dx, dz) == (0, 0):

                @pl.when(away)
                def _(rc=rc):
                    rc.wait_send()
            else:
                rc.wait_send()
    remote(meta, meta, msem.at[0, 1], msem.at[1, 0], here_dev).wait_send()

    @pl.when(jnp.logical_not(here))
    def _():
        remote(meta, meta, msem.at[0, 0], msem.at[1, 0], here_dev).wait_send()


def dot_t(a, b):
    return lax.dot_general(a, b, (((1,), (1,)), ((), ())), preferred_element_type=f32)


def dot(a, b):
    return jnp.dot(a, b, preferred_element_type=f32)


def tables(rmeta, pool, group0, idx, slot):
    @pl.loop(0, 16)
    def _(n):
        u, i = n // 8, n % 8
        g = group0 + u
        loc = [(i + rmeta[u, i, j]) % 8 for j in range(4)]
        for j in range(4):
            idx[n * NKEY + j] = u * 8 + loc[j]
        for kb in range(8):
            s = jnp.int32(ZERO)
            for j in range(4):
                s = jnp.where(loc[j] == kb, n * NKEY + j, s)
            slot[n * TILES + kb] = s
        for b in range(2):
            base = (1 - u) * 8 if b == 0 else 16 + u * 8
            picks = [rmeta[u, i, 4 + b * 4 + t] for t in range(4)]
            for t in range(4):
                idx[n * NKEY + 4 + b * 4 + t] = base + pool[(g * 2 + b) * 5 + picks[t]]
            for p in range(5):
                s = jnp.int32(ZERO)
                for t in range(4):
                    s = jnp.where(picks[t] == p, n * NKEY + 4 + b * 4 + t, s)
                slot[n * TILES + 8 + b * 5 + p] = s


def pool_place(pool, group, b, kb, none):
    s = jnp.int32(none)
    for p in range(5):
        s = jnp.where(pool[(group * 2 + b) * 5 + p] == kb, p, s)
    return s


def attend_block(n, idx, qd, kv, kt, sp, x, dq):
    ids = [idx[n * NKEY + j] for j in range(NKEY)]
    sp[...] = dot_t(jnp.concatenate([kv[r] for r in ids], axis=0), qd[n])
    m = jnp.full((8, 128), -jnp.inf, f32)
    for j in range(NKEY):
        s = sp[j * 128 : (j + 1) * 128, 0:128].reshape(16, 8, 128)
        m = jnp.maximum(m, jnp.max(s, axis=0))
    m = jnp.max(m, axis=0, keepdims=True) * SCALE
    den = jnp.zeros((8, 128), f32)
    num = jnp.zeros((8, 128), f32)
    for j in range(NKEY):
        s = sp[j * 128 : (j + 1) * 128, 0:128]
        p = sp[j * 128 : (j + 1) * 128, 128:256]
        e = jnp.exp(s * SCALE - m)
        sp[j * 128 : (j + 1) * 128, 0:128] = e
        den = den + jnp.sum(e.reshape(16, 8, 128), axis=0)
        num = num + jnp.sum((e * p).reshape(16, 8, 128), axis=0)
    rden = 1.0 / jnp.sum(den, axis=0, keepdims=True)
    delta = jnp.sum(num, axis=0, keepdims=True) * rden
    rscaled = rden * SCALE
    for j in range(NKEY):
        e = sp[j * 128 : (j + 1) * 128, 0:128]
        p = sp[j * 128 : (j + 1) * 128, 128:256]
        x[n * NKEY + j, :, 128:256] = (e * rden).astype(bf16)
        x[n * NKEY + j, :, 0:128] = ((e * rscaled) * (p - delta)).astype(bf16)
    kts = jnp.concatenate([kt[r] for r in ids], axis=1)
    ds = jnp.concatenate([x[n * NKEY + j, :, 0:128] for j in range(NKEY)], axis=0)
    dq[n] = dot(kts, ds).T.astype(bf16)


def compute_kernel(rmeta, pool, qd, kv, dq, own, part, idx, slot, kt, x, sp, acc):
    ctx, xb, z, core = place()
    group0 = (ctx // 4) * 4 + core * 2
    tables(rmeta, pool, group0, idx, slot)
    x[ZERO] = jnp.zeros((128, 256), bf16)
    acc[26] = jnp.zeros((128, 256), f32)

    @pl.loop(0, 32)
    def _(b):
        kt[b] = kv[b, :, 0:128].T

    @pl.loop(0, 16)
    def _(n):
        attend_block(n, idx, qd, kv, kt, sp, x, dq)

    def tile_sum(u, t):
        rows = jnp.concatenate([x[slot[(u * 8 + i) * TILES + t]] for i in range(8)], axis=1)
        return dot(rows, qd[pl.ds(u * 8, 8)].reshape(2048, 256))

    for u in range(2):

        @pl.loop(0, 13)
        def _(t):
            acc[u * 13 + t] = tile_sum(u, t)

        @pl.loop(0, 5)
        def _(p):
            part[u * 5 + p] = tile_sum(u, 13 + p)

    for u in range(2):

        @pl.loop(0, 8)
        def _(kb):
            p = pool_place(pool, group0 + 1 - u, 0, kb, 18 - (1 - u) * 13)
            own[u * 8 + kb] = acc[u * 13 + kb] + acc[(1 - u) * 13 + 8 + p]


def gather_kernel(pool, dq, own, part, oq, ok, ov, recv, fin, ssem, rsem, psem):
    ctx, xb, z, core = place()
    group0 = (ctx // 4) * 4 + core * 2
    recv[10] = jnp.zeros((128, 256), f32)
    away = core != xb
    others = []
    for s in range(8):
        zs = (z + s) % 8
        for x in range(2):
            cond = jnp.logical_or(away, jnp.logical_or(zs != z, xb != x))
            others.append((cond, (x, zs, xb)))
    others.append((jnp.logical_not(away), (xb, z, 1 - core)))
    greet(ctx, others, jnp.where(away, 17, 15))
    here_dev = device(ctx, xb, z, 1 - core)
    swap = remote(part, recv.at[0:10], psem.at[0], psem.at[1], here_dev)
    swap.start()
    cols = pl.ds(pl.multiple_of((xb * 8 + z) * 128, 128), 128)
    order = [(dz, c) for dz in (4, 3, 5, 2, 6, 1, 7, 0) for c in (0, 1)]
    outs = (oq, ok, ov)
    sem_row = xb * 8 + z

    def src(a, n):
        if a == 0:
            return dq.at[n]
        return fin.at[n, :, (a - 1) * 128 : a * 128]

    def send(a, o):
        dz, c = order[o]
        zd = (z + dz) % 8
        n = zd * 2 + c
        dst = outs[a].at[:, cols]
        rc = remote(src(a, n), dst, ssem.at[a, o], rsem.at[a, sem_row], device(ctx, core, zd, c))
        if dz == 0:
            here = jnp.logical_and(jnp.logical_not(away), core == c)

            @pl.when(jnp.logical_not(here))
            def _():
                rc.start()

            @pl.when(here)
            def _():
                pltpu.make_async_copy(src(a, n), dst, rsem.at[a, sem_row]).start()
        else:
            rc.start()

    for o in range(16):
        send(0, o)
    swap.wait()
    for o in range(16):
        dz, c = order[o]
        n = ((z + dz) % 8) * 2 + c
        u = n // 8
        p = pool_place(pool, (ctx // 4) * 4 + (1 - core) * 2 + u, 1, n % 8, 10 - u * 5)
        fin[n] = (own[n] + recv[u * 5 + p]).astype(bf16)
        send(1, o)
        send(2, o)
    for a in range(3):
        for r in range(16):
            ref = outs[a].at[:, r * 128 : (r + 1) * 128]
            remote(ref, ref, ssem.at[a, 0], rsem.at[a, r], here_dev).wait_recv()
    for o in range(16):
        dz, c = order[o]
        for a in range(3):
            rc = remote(dq.at[0], dq.at[0], ssem.at[a, o], rsem.at[a, 0], here_dev)
            if dz == 0:

                @pl.when(jnp.logical_or(away, core != c))
                def _(rc=rc):
                    rc.wait_send()
            else:
                rc.wait_send()


def per_device(q, k, v, g, local_offsets, partner_pool, partner_picks):
    hbm = pl.BlockSpec(memory_space=pltpu.HBM)
    vm = pl.BlockSpec(memory_space=pltpu.VMEM)
    sm = pl.BlockSpec(memory_space=pltpu.SMEM)
    dma = pltpu.SemaphoreType.DMA
    meta = jnp.concatenate([local_offsets, partner_picks.reshape(8, 8)], axis=1)
    meta = jnp.pad(meta, ((0, 0), (0, 116)))
    pool = partner_pool.reshape(-1)
    sds = jax.ShapeDtypeStruct
    qd, kv, rmeta = pl.pallas_call(
        scatter_kernel,
        name="scatter",
        out_shape=(
            sds((16, 256, 256), bf16),
            sds((32, 128, 256), bf16),
            sds((2, 8, 128), jnp.int32),
        ),
        in_specs=[hbm] * 4 + [vm],
        out_specs=(vm, vm, vm),
        scratch_shapes=[dma((4, 16)), dma((4, 16)), dma((2,)), dma((2, 2))],
        compiler_params=pltpu.CompilerParams(collective_id=0, has_side_effects=True),
    )(q, k, v, g, meta)
    dq, own, part = pl.pallas_call(
        compute_kernel,
        name="compute",
        out_shape=(
            sds((16, 128, 128), bf16),
            sds((16, 128, 256), f32),
            sds((10, 128, 256), f32),
        ),
        in_specs=[sm, sm, vm, vm],
        out_specs=(vm, vm, vm),
        scratch_shapes=[
            pltpu.SMEM((16 * NKEY,), jnp.int32),
            pltpu.SMEM((16 * TILES,), jnp.int32),
            pltpu.VMEM((32, 128, 128), bf16),
            pltpu.VMEM((ZERO + 1, 128, 256), bf16),
            pltpu.VMEM((NKEY * 128, 256), f32),
            pltpu.VMEM((27, 128, 256), f32),
        ],
        compiler_params=pltpu.CompilerParams(vmem_limit_bytes=58 << 20),
    )(rmeta, pool, qd, kv)
    return pl.pallas_call(
        gather_kernel,
        name="gather",
        out_shape=tuple(sds((128, 2048), bf16) for _ in range(3)),
        in_specs=[sm, vm, vm, vm],
        out_specs=(hbm, hbm, hbm),
        scratch_shapes=[
            pltpu.VMEM((11, 128, 256), f32),
            pltpu.VMEM((16, 128, 256), bf16),
            dma((3, 16)),
            dma((3, 16)),
            dma((2,)),
        ],
        compiler_params=pltpu.CompilerParams(collective_id=1, has_side_effects=True),
    )(pool, dq, own, part)


def solution(mesh):
    tok = P(("ctx", "head"), None)
    return jax.shard_map(
        per_device,
        mesh=mesh,
        in_specs=(tok, tok, tok, tok, P("ctx", None), P(), P("ctx", None, None)),
        out_specs=(tok, tok, tok),
        check_vma=False,
    )
```

time: 507 us -> 155 us (0.31)
  waiting for transfers between devices: 164 us -> 0 us
  Pallas kernels: 0 us -> 146 us
  local copies, waits for them, and re-layouts: 134 us -> 8.24 us
  other arithmetic: 92.3 us -> 0.08 us
  matrix products: 57.2 us -> 0 us
  starting transfers between devices: 51.7 us -> 0 us
    pallas_call x0 -> x3, Pallas kernels: none -> 146 us  [the longest x1 61 us: per_device(): pl.pallas_call(scatter_kernel, name='scatter', out_shape=(sds((16, 256, 2...]
    ppermute x8 -> x0, waiting for transfers between devices: 115 us -> none  [swapped(): lax.ppermute(value, axis, [(i, i ^ 1 << distance) for i in range(lax.axis...]
    scatter-add x12 -> x0, other arithmetic: 85.6 us -> none  [the longest x4 39.1 us: attend(): acc_value.at[flat_index]]
    reshape x24 -> x2, local copies, waits for them, and re-layouts: 51 us -> 1.48 us  [the longest x1 0.75 us: per_device(): meta = jnp.concatenate([local_offsets, partner_picks.reshape(8, 8)], axis=1)]
    all_to_all x7 -> x0, waiting for transfers between devices: 49.1 us -> none  [the longest x1 13.4 us: per_device(): lax.all_to_all(key_vecs, 'head', split_axis=1, concat_axis=0, tiled=True)]
    dot_general x16 -> x0, matrix products: 42.2 us -> none  [the longest x4 12.8 us: attend(): jnp.einsum('ghqk,gqhd->gkhd', weights_half, grad_part, preferred_element_...]
    transpose x8 -> x0, local copies, waits for them, and re-layouts: 39.5 us -> none  [the longest x4 22.9 us: attend(): jnp.einsum('ghqk,gqhd->gkhd', weights_half, grad_part, preferred_element_...]
    all_to_all x7 -> x0, starting transfers between devices: 37.3 us -> none  [the longest x1 7.39 us: per_device(): lax.all_to_all(queries, 'head', split_axis=1, concat_axis=0, tiled=True)]
  transfers between devices with their start and end apart: 15 -> 0, of which waited for: 9 -> 0; matrix products, arithmetic and copies ran while one was open for 7% -> 0% of each run, Pallas kernels for 0% -> 0%
where the time goes in v1:
time: 155 us
  Pallas kernels  146 us (94%)
  local copies, waits for them, and re-layouts  8.24 us (5%)
    pallas_call x1, Pallas kernels, per_device(): pl.pallas_call(scatter_kernel, name='scatter', out_shape=(sds((16, 256, 2...  61 us
    pallas_call x1, Pallas kernels, per_device(): pl.pallas_call(gather_kernel, name='gather', out_shape=tuple((sds((128, 2...  44.3 us
    pallas_call x1, Pallas kernels, per_device(): pl.pallas_call(compute_kernel, name='compute', out_shape=(sds((16, 128, 1...  40.8 us
    unnamed x7, local copies, waits for them, and re-layouts  6.16 us

profile of v1, /device:TPU:1, one launch (start us, length us, event | category | flops | bytes accessed | tf_op | source)
XLA Modules:
  0.0 155.1 jit_solution(2330038134922183807)
XLA Ops:
  0.6 0.8 copy.13
  1.4 0.8 copy.14
  2.1 0.1 pad_add_fusion
  2.2 0.6 pad.4.meta
  2.8 0.8 copy.12
  3.6 0.7 reshape.12.pool
  4.3 61.0 %scatter.1 = (bf16[16,256,256]{2,1,0:T(8,128)(2,1)}, bf16[32,128,256]{2,1,0:T(8,128)(2,1)}, s32[2,8,128]{2,1,0:T(8,128)}) custom-call(bf16[128,2048]{1,0:T(8,128)(2,1)} %q.1, bf16[128,2048]{1,0:T(8,128)(2,1)} %k.1, bf16[128,2048]{1,0:T(8,128)(2,1)} %v.1, bf16[128,2048]{1,0:T(8,128)(2,1)} %g.1, s32[8,128]{1,0:T(8,128)} %pad.4.meta), custom_call_target="tpu_custom_call" | custom-call | tf_op jit(solution)/shard_map/scatter/pallas_call | solution.py:334
  65.3 40.8 %compute.1 = (bf16[16,128,128]{2,1,0:T(8,128)(2,1)}, f32[16,128,256]{2,1,0:T(8,128)}, f32[10,128,256]{2,1,0:T(8,128)}) custom-call(s32[2,8,128]{2,1,0:T(8,128)} %get-tuple-element.9.rmeta, s32[320]{0:T(512)} %reshape.12.pool, bf16[16,256,256]{2,1,0:T(8,128)(2,1)} %get-tuple-element.10.qd, bf16[32,128,256]{2,1,0:T(8,128)(2,1)} %get-tuple-element.11.kv), custom_call_target="tpu_custom_call" | custom-call | tf_op jit(solution)/shard_map/compute/pallas_call | solution.py:347
  106.1 44.3 %gather.1 = (bf16[128,2048]{1,0:T(8,128)(2,1)}, bf16[128,2048]{1,0:T(8,128)(2,1)}, bf16[128,2048]{1,0:T(8,128)(2,1)}) custom-call(s32[320]{0:T(512)} %reshape.12.pool, bf16[16,128,128]{2,1,0:T(8,128)(2,1)} %get-tuple-element.12.dq, f32[16,128,256]{2,1,0:T(8,128)} %get-tuple-element.13.own, f32[10,128,256]{2,1,0:T(8,128)} %get-tuple-element.14.part), custom_call_target="tpu_custom_call" | custom-call | tf_op jit(solution)/shard_map/gather/pallas_call | solution.py:367
  150.5 0.0 copy-start
  150.5 1.9 %copy.18 = bf16[128,2048]{1,0:T(8,128)(2,1)} copy(bf16[128,2048]{1,0:T(8,128)(2,1)} %get-tuple-element.18) | data formatting | bytes 1048576
  152.4 1.9 %copy.19 = bf16[128,2048]{1,0:T(8,128)(2,1)} copy(bf16[128,2048]{1,0:T(8,128)(2,1)} %get-tuple-element.19) | data formatting | bytes 1048576
  154.3 0.0 copy-done
  154.3 0.8 copy.20
Async XLA Ops:
  150.5 3.8 %copy-start = (bf16[128,2048]{1,0:T(8,128)(2,1)S(1)}, bf16[128,2048]{1,0:T(8,128)(2,1)}, u32[]{:S(2)}) copy-start(bf16[128,2048]{1,0:T(8,128)(2,1)} %get-tuple-element.20) | copy-start | bytes 1572868

commit v2 on v0

v2 whole, which is shorter than its diff:
```python
import jax
import jax.numpy as jnp
from jax import lax
from jax.experimental import pallas as pl
from jax.experimental.pallas import tpu as pltpu
from jax.sharding import PartitionSpec as P

MESH = pl.DeviceIdType.MESH
DH = 128
BLK = 128
NKEY = 12
TILES = 18
ZERO = 16 * NKEY
SCALE = DH**-0.5
f32 = jnp.float32
bf16 = jnp.bfloat16
SHIFTS = (0, 1, 7, 2, 6, 3, 5, 4)
ORDER = [(dx, dz) for dz in SHIFTS for dx in (0, 1)]


def place():
    ctx = lax.axis_index("ctx")
    head = lax.axis_index("head")
    return ctx, (ctx // 2) % 2, (ctx % 2) * 4 + head // 2, head % 2


def device(ctx, xb, z, core):
    return ((ctx // 4) * 4 + xb * 2 + z // 4, (z % 4) * 2 + core)


def remote(src, dst, ssem, rsem, dev):
    return pltpu.make_async_remote_copy(
        src_ref=src, dst_ref=dst, send_sem=ssem, recv_sem=rsem, device_id=dev, device_id_type=MESH
    )


def dot_t(a, b):
    return lax.dot_general(a, b, (((1,), (1,)), ((), ())), preferred_element_type=f32)


def dot(a, b):
    return jnp.dot(a, b, preferred_element_type=f32)


def tables(offs, picks, pool, group0, idx, slot):
    @pl.loop(0, 16)
    def _(n):
        u, i = n // 8, n % 8
        g = group0 + u
        loc = [(i + offs[u, j, i]) % 8 for j in range(4)]
        for j in range(4):
            idx[n * NKEY + j] = u * 8 + loc[j]
        for kb in range(8):
            s = jnp.int32(ZERO)
            for j in range(4):
                s = jnp.where(loc[j] == kb, n * NKEY + j, s)
            slot[n * TILES + kb] = s
        for b in range(2):
            base = (1 - u) * 8 if b == 0 else 16 + u * 8
            picked = [picks[u, b, t, i] for t in range(4)]
            for t in range(4):
                idx[n * NKEY + 4 + b * 4 + t] = base + pool[picked[t], b, g]
            for p in range(5):
                s = jnp.int32(ZERO)
                for t in range(4):
                    s = jnp.where(picked[t] == p, n * NKEY + 4 + b * 4 + t, s)
                slot[n * TILES + 8 + b * 5 + p] = s


def pool_place(pool, group, b, kb, none):
    s = jnp.int32(none)
    for p in range(5):
        s = jnp.where(pool[p, b, group] == kb, p, s)
    return s


def attend_block(n, idx, qd, kv, kt, sp, x, dq):
    ids = [idx[n * NKEY + j] for j in range(NKEY)]
    sp[...] = dot_t(jnp.concatenate([kv[r] for r in ids], axis=0), qd[n])
    m = jnp.full((8, 128), -jnp.inf, f32)
    for j in range(NKEY):
        s = sp[j * 128 : (j + 1) * 128, 0:128].reshape(16, 8, 128)
        m = jnp.maximum(m, jnp.max(s, axis=0))
    m = jnp.max(m, axis=0, keepdims=True) * SCALE
    den = jnp.zeros((8, 128), f32)
    num = jnp.zeros((8, 128), f32)
    for j in range(NKEY):
        s = sp[j * 128 : (j + 1) * 128, 0:128]
        p = sp[j * 128 : (j + 1) * 128, 128:256]
        e = jnp.exp(s * SCALE - m)
        sp[j * 128 : (j + 1) * 128, 0:128] = e
        den = den + jnp.sum(e.reshape(16, 8, 128), axis=0)
        num = num + jnp.sum((e * p).reshape(16, 8, 128), axis=0)
    rden = 1.0 / jnp.sum(den, axis=0, keepdims=True)
    delta = jnp.sum(num, axis=0, keepdims=True) * rden
    rscaled = rden * SCALE
    for j in range(NKEY):
        e = sp[j * 128 : (j + 1) * 128, 0:128]
        p = sp[j * 128 : (j + 1) * 128, 128:256]
        x[n * NKEY + j, :, 128:256] = (e * rden).astype(bf16)
        x[n * NKEY + j, :, 0:128] = ((e * rscaled) * (p - delta)).astype(bf16)
    kts = jnp.concatenate([kt[r] for r in ids], axis=1)
    ds = jnp.concatenate([x[n * NKEY + j, :, 0:128] for j in range(NKEY)], axis=0)
    dq[n] = dot(kts, ds).T.astype(bf16)


def shift(o):
    return lax.rem(o, 2) * ((o + 1) // 2) + (1 - lax.rem(o, 2)) * lax.rem(8 - o // 2, 8)


def kernel(
    q, k, v, g, offsets, partner_picks, pool,
    oq, ok, ov,
    qd, kv, kt, x, sp0, sp1, dq, part, near, recv, fin,
    voffs, vpicks, offs, picks, idx, slot,
    ssem, rsem, fsem, msem, lsem, osem, orsem, psem,
):
    ctx, xb, z, core = place()
    group0 = (ctx // 4) * 4 + core * 2
    away = core != xb
    at_home = core == xb
    here_dev = device(ctx, xb, z, 1 - core)
    barrier = pltpu.get_barrier_semaphore()
    for dx in range(2):
        for dz in SHIFTS:
            for dc in range(2):
                if (dx, dz, dc) != (0, 0, 0):
                    dev = device(ctx, xb ^ dx, (z + dz) % 8, core ^ dc)
                    pl.semaphore_signal(barrier, 1, device_id=dev, device_id_type=MESH)
    qd[:, 0:128, 128:256] = jnp.zeros((16, 128, 128), bf16)
    qd[:, 128:256, 0:128] = jnp.zeros((16, 128, 128), bf16)
    pl.semaphore_wait(barrier, 31)

    mine = (z % 4) * 2 + core
    mrow = z // 4
    small = ((offsets, voffs, offs), (partner_picks, vpicks, picks))
    meta_here = jnp.logical_and(at_home, mine == z)
    for dx in (0, 1):
        for b, (src, dst, _) in enumerate(small):
            rc = remote(
                src, dst.at[mrow], msem.at[b, dx], msem.at[b, 2 + mrow],
                device(ctx, xb ^ dx, mine, xb),
            )
            if dx == 1:
                rc.start()
            else:

                @pl.when(jnp.logical_not(meta_here))
                def _(rc=rc):
                    rc.start()

                @pl.when(meta_here)
                def _(src=src, dst=dst, b=b):
                    pltpu.make_async_copy(src, dst.at[mrow], msem.at[b, 2 + mrow]).start()

    slot_here = z * 2 + core
    srcs = (k, v, q, g)

    def place_of(a, n):
        if a == 0:
            return kv.at[n, :, 0:128]
        if a == 1:
            return kv.at[n, :, 128:256]
        if a == 2:
            return qd.at[n, 0:128, 0:128]
        return qd.at[n, 128:256, 128:256]

    for a0 in (0, 2):
        for o, (dx, dz) in enumerate(ORDER):
            xd, zd = xb ^ dx, (z + dz) % 8
            cols = pl.ds(pl.multiple_of((xd * 8 + zd) * 128, 128), 128)
            for a in (a0, a0 + 1):
                src = srcs[a].at[:, cols]
                dst = place_of(a, slot_here)
                rc = remote(
                    src, dst, ssem.at[a, o], rsem.at[a, slot_here], device(ctx, xd, zd, xb)
                )
                if (dx, dz) == (0, 0):

                    @pl.when(away)
                    def _(rc=rc):
                        rc.start()

                    @pl.when(at_home)
                    def _(src=src, dst=dst, a=a):
                        pltpu.make_async_copy(src, dst, rsem.at[a, slot_here]).start()
                else:
                    rc.start()

    def arrived(a, n):
        ref = place_of(a, n)
        remote(ref, ref, ssem.at[a, 0], rsem.at[a, n], here_dev).wait_recv()

    for n in range(2):
        for b, (src, dst, _) in enumerate(small):
            remote(src, dst.at[n], msem.at[b, 0], msem.at[b, 2 + n], here_dev).wait_recv()
    for b, (_, src, dst) in enumerate(small):
        local = pltpu.make_async_copy(src, dst, lsem.at[b])
        local.start()
        local.wait()
    tables(offs, picks, pool, group0, idx, slot)
    x[ZERO] = jnp.zeros((128, 256), bf16)
    near[10] = jnp.zeros((128, 256), f32)
    recv[10] = jnp.zeros((128, 256), f32)

    def forward(n):
        return remote(kv.at[n], kv.at[16 + n], fsem.at[0, n], fsem.at[1, n], here_dev)

    @pl.loop(0, 8)
    def _(o):
        zs = (z + 8 - shift(o)) % 8
        for c in range(2):
            n = zs * 2 + c
            arrived(0, n)
            arrived(1, n)
            forward(n).start()
            kt[n] = kv[n, :, 0:128].T

    @pl.loop(0, 8)
    def _(o):
        zs = (z + 8 - shift(o)) % 8
        for c in range(2):
            n = zs * 2 + c
            forward(n).wait_recv()
            kt[16 + n] = kv[16 + n, :, 0:128].T

    cols = pl.ds(pl.multiple_of((xb * 8 + z) * 128, 128), 128)
    row = xb * 8 + z
    outs = (oq, ok, ov)

    def result(a, n):
        if a == 0:
            return dq.at[n]
        return fin.at[n, :, (a - 1) * 128 : a * 128]

    def out_copy(a, n, zs, c):
        return remote(
            result(a, n), outs[a].at[:, cols], osem.at[a, n], orsem.at[a, row],
            device(ctx, core, zs, c),
        )

    def stays(zs, c):
        return jnp.logical_and(at_home, jnp.logical_and(zs == z, core == c))

    def send(a, n, zs, c):
        @pl.when(jnp.logical_not(stays(zs, c)))
        def _():
            out_copy(a, n, zs, c).start()

        @pl.when(stays(zs, c))
        def _():
            pltpu.make_async_copy(result(a, n), outs[a].at[:, cols], orsem.at[a, row]).start()

    @pl.loop(0, 8)
    def _(o):
        zs = (z + 8 - shift(o)) % 8
        for c in range(2):
            arrived(2, zs * 2 + c)
            arrived(3, zs * 2 + c)
        for c, sp in ((0, sp0), (1, sp1)):
            attend_block(zs * 2 + c, idx, qd, kv, kt, sp, x, dq)
        for c in range(2):
            send(0, zs * 2 + c, zs, c)

    def tile_sum(u, t):
        rows = jnp.concatenate([x[slot[(u * 8 + i) * TILES + t]] for i in range(8)], axis=1)
        return dot(rows, qd[pl.ds(u * 8, 8)].reshape(2048, 256))

    @pl.loop(0, 10)
    def _(t):
        part[t] = tile_sum(t // 5, 13 + t % 5)

    swap = remote(part, recv.at[0:10], psem.at[0], psem.at[1], here_dev)
    swap.start()

    @pl.loop(0, 10)
    def _(t):
        near[t] = tile_sum(t // 5, 8 + t % 5)

    swap.wait()

    @pl.loop(0, 8)
    def _(o):
        zs = (z + 8 - shift(o)) % 8
        u = zs // 4
        for c in range(2):
            n = zs * 2 + c
            p = (1 - u) * 5 + pool_place(pool, group0 + 1 - u, 0, n % 8, 10 - (1 - u) * 5)
            r = u * 5 + pool_place(
                pool, (ctx // 4) * 4 + (1 - core) * 2 + u, 1, n % 8, 10 - u * 5
            )
            fin[n] = (tile_sum(u, n % 8) + near[p] + recv[r]).astype(bf16)
            send(1, n, zs, c)
            send(2, n, zs, c)

    @pl.loop(0, 16)
    def _(r):
        for a in range(3):
            ref = outs[a].at[:, pl.ds(pl.multiple_of(r * 128, 128), 128)]
            remote(ref, ref, osem.at[a, 0], orsem.at[a, r], here_dev).wait_recv()

    for o, (dx, dz) in enumerate(ORDER):
        for a in range(4):
            src = srcs[a].at[:, 0:128]
            rc = remote(src, src, ssem.at[a, o], rsem.at[a, 0], here_dev)
            if (dx, dz) == (0, 0):

                @pl.when(away)
                def _(rc=rc):
                    rc.wait_send()
            else:
                rc.wait_send()
    for b, (src, dst, _) in enumerate(small):
        remote(src, dst.at[0], msem.at[b, 1], msem.at[b, 2], here_dev).wait_send()

        @pl.when(jnp.logical_not(meta_here))
        def _(src=src, dst=dst, b=b):
            remote(src, dst.at[0], msem.at[b, 0], msem.at[b, 2], here_dev).wait_send()

    @pl.loop(0, 8)
    def _(zs):
        for c in range(2):
            n = zs * 2 + c
            forward(n).wait_send()

            @pl.when(jnp.logical_not(stays(zs, c)))
            def _(n=n, zs=zs, c=c):
                for a in range(3):
                    out_copy(a, n, zs, c).wait_send()


def per_device(q, k, v, g, local_offsets, partner_pool, partner_picks):
    hbm = pl.BlockSpec(memory_space=pltpu.HBM)
    sm = pl.BlockSpec(memory_space=pltpu.SMEM)
    dma = pltpu.SemaphoreType.DMA
    i32 = jnp.int32
    return pl.pallas_call(
        kernel,
        name="butterfly",
        out_shape=tuple(jax.ShapeDtypeStruct((128, 2048), bf16) for _ in range(3)),
        in_specs=[hbm] * 6 + [sm],
        out_specs=(hbm, hbm, hbm),
        scratch_shapes=[
            pltpu.VMEM((16, 256, 256), bf16),
            pltpu.VMEM((32, 128, 256), bf16),
            pltpu.VMEM((32, 128, 128), bf16),
            pltpu.VMEM((ZERO + 1, 128, 256), bf16),
            pltpu.VMEM((NKEY * 128, 256), f32),
            pltpu.VMEM((NKEY * 128, 256), f32),
            pltpu.VMEM((16, 128, 128), bf16),
            pltpu.VMEM((10, 128, 256), f32),
            pltpu.VMEM((11, 128, 256), f32),
            pltpu.VMEM((11, 128, 256), f32),
            pltpu.VMEM((16, 128, 256), bf16),
            pltpu.VMEM((2, 4, 8), i32),
            pltpu.VMEM((2, 2, 4, 8), i32),
            pltpu.SMEM((2, 4, 8), i32),
            pltpu.SMEM((2, 2, 4, 8), i32),
            pltpu.SMEM((16 * NKEY,), i32),
            pltpu.SMEM((16 * TILES,), i32),
            dma((4, 16)),
            dma((4, 16)),
            dma((2, 16)),
            dma((2, 4)),
            dma((2,)),
            dma((3, 16)),
            dma((3, 16)),
            dma((2,)),
        ],
        compiler_params=pltpu.CompilerParams(
            collective_id=0, has_side_effects=True, vmem_limit_bytes=58 << 20
        ),
    )(q, k, v, g, local_offsets.T, partner_picks.transpose(1, 2, 0), partner_pool.transpose(2, 1, 0))


def solution(mesh):
    tok = P(("ctx", "head"), None)
    return jax.shard_map(
        per_device,
        mesh=mesh,
        in_specs=(tok, tok, tok, tok, P("ctx", None), P(), P("ctx", None, None)),
        out_specs=(tok, tok, tok),
        check_vma=False,
    )
```

time: 507 us -> 107 us (0.21)
  the two profiles are of different devices: /device:TPU:1 before, /device:TPU:81 now
where the time goes in v2:
time: 107 us
  Pallas kernels  103 us (96%)
  local copies, waits for them, and re-layouts  3.97 us (4%)
    pallas_call x1, Pallas kernels, per_device(): pl.pallas_call(kernel, name='butterfly', out_shape=tuple((jax.ShapeDtypeS...  103 us
    unnamed x7, local copies, waits for them, and re-layouts  3.97 us

profile of v2, /device:TPU:81, one launch (start us, length us, event | category | flops | bytes accessed | tf_op | source)
XLA Modules:
  0.0 107.2 jit_solution(298473048096797006)
XLA Ops:
  0.6 102.6 %butterfly.1 = (bf16[128,2048]{1,0:T(8,128)(2,1)}, bf16[128,2048]{1,0:T(8,128)(2,1)}, bf16[128,2048]{1,0:T(8,128)(2,1)}) custom-call(bf16[128,2048]{1,0:T(8,128)(2,1)} %q.1, bf16[128,2048]{1,0:T(8,128)(2,1)} %k.1, bf16[128,2048]{1,0:T(8,128)(2,1)} %v.1, bf16[128,2048]{1,0:T(8,128)(2,1)} %g.1, s32[4,8]{1,0:T(4,128)} %bitcast.5, s32[2,4,8]{2,1,0:T(4,128)} %bitcast.4, ...), custom_call_target="tpu_custom_call" | custom-call | tf_op jit(solution)/shard_map/butterfly/pallas_call | solution.py:337
  103.2 0.0 copy-start.1
  103.2 1.9 %copy.13 = bf16[128,2048]{1,0:T(8,128)(2,1)} copy(bf16[128,2048]{1,0:T(8,128)(2,1)} %get-tuple-element.6) | data formatting | bytes 1048576
  105.2 0.0 copy-done.1
  105.2 0.0 copy-start
  105.2 0.8 copy.14
  106.0 0.4 copy-done
  106.4 0.8 copy.15
Async XLA Ops:
  103.2 2.0 %copy-start.1 = (bf16[128,2048]{1,0:T(8,128)(2,1)S(1)}, bf16[128,2048]{1,0:T(8,128)(2,1)}, u32[]{:S(2)}) copy-start(bf16[128,2048]{1,0:T(8,128)(2,1)} %get-tuple-element.7) | copy-start | bytes 1572868
  105.2 1.2 %copy-start = (bf16[128,2048]{1,0:T(8,128)(2,1)S(1)}, bf16[128,2048]{1,0:T(8,128)(2,1)}, u32[]{:S(2)}) copy-start(bf16[128,2048]{1,0:T(8,128)(2,1)} %get-tuple-element.8) | copy-start | bytes 1572868

commit v3 on v2

--- a/solution.py
+++ b/solution.py
@@ -74,9 +74,12 @@
     return s
 
 
-def attend_block(n, idx, qd, kv, kt, sp, x, dq):
-    ids = [idx[n * NKEY + j] for j in range(NKEY)]
-    sp[...] = dot_t(jnp.concatenate([kv[r] for r in ids], axis=0), qd[n])
+def scores(n, idx, qd, kv, sp):
+    rows = jnp.concatenate([kv[idx[n * NKEY + j]] for j in range(NKEY)], axis=0)
+    sp[...] = dot_t(rows, qd[n])
+
+
+def softmax_grads(n, sp, x):
     m = jnp.full((8, 128), -jnp.inf, f32)
     for j in range(NKEY):
         s = sp[j * 128 : (j + 1) * 128, 0:128].reshape(16, 8, 128)
@@ -99,9 +102,13 @@
         p = sp[j * 128 : (j + 1) * 128, 128:256]
         x[n * NKEY + j, :, 128:256] = (e * rden).astype(bf16)
         x[n * NKEY + j, :, 0:128] = ((e * rscaled) * (p - delta)).astype(bf16)
-    kts = jnp.concatenate([kt[r] for r in ids], axis=1)
+
+
+def query_grad(n, idx, kv, x, dq):
+    keys = jnp.concatenate([kv[idx[n * NKEY + j], :, 0:128] for j in range(NKEY)], axis=0)
     ds = jnp.concatenate([x[n * NKEY + j, :, 0:128] for j in range(NKEY)], axis=0)
-    dq[n] = dot(kts, ds).T.astype(bf16)
+    out = lax.dot_general(ds, keys, (((0,), (0,)), ((), ())), preferred_element_type=f32)
+    dq[n] = out.astype(bf16)
 
 
 def shift(o):
@@ -111,7 +118,7 @@
 def kernel(
     q, k, v, g, offsets, partner_picks, pool,
     oq, ok, ov,
-    qd, kv, kt, x, sp0, sp1, dq, part, near, recv, fin,
+    qd, kv, x, sp0, sp1, dq, part, near, own, recv, fin,
     voffs, vpicks, offs, picks, idx, slot,
     ssem, rsem, fsem, msem, lsem, osem, orsem, psem,
 ):
@@ -121,15 +128,23 @@
     at_home = core == xb
     here_dev = device(ctx, xb, z, 1 - core)
     barrier = pltpu.get_barrier_semaphore()
-    for dx in range(2):
-        for dz in SHIFTS:
-            for dc in range(2):
-                if (dx, dz, dc) != (0, 0, 0):
-                    dev = device(ctx, xb ^ dx, (z + dz) % 8, core ^ dc)
-                    pl.semaphore_signal(barrier, 1, device_id=dev, device_id_type=MESH)
+    for dz in SHIFTS[::-1]:
+        zd = (z + dz) % 8
+        targets = [(core, 1 - xb), (1 - core, xb), (core, xb)]
+        for xd, cd in targets[: 3 if dz else 2]:
+            pl.semaphore_signal(
+                barrier, 1, device_id=device(ctx, xd, zd, cd), device_id_type=MESH
+            )
+
+    @pl.when(away)
+    def _():
+        pl.semaphore_signal(
+            barrier, 1, device_id=device(ctx, core, z, xb), device_id_type=MESH
+        )
+
     qd[:, 0:128, 128:256] = jnp.zeros((16, 128, 128), bf16)
     qd[:, 128:256, 0:128] = jnp.zeros((16, 128, 128), bf16)
-    pl.semaphore_wait(barrier, 31)
+    pl.semaphore_wait(barrier, 23 + away.astype(jnp.int32))
 
     mine = (z % 4) * 2 + core
     mrow = z // 4
@@ -200,7 +215,8 @@
         local.wait()
     tables(offs, picks, pool, group0, idx, slot)
     x[ZERO] = jnp.zeros((128, 256), bf16)
-    near[10] = jnp.zeros((128, 256), f32)
+    near[...] = jnp.zeros((11, 128, 256), f32)
+    part[...] = jnp.zeros((10, 128, 256), f32)
     recv[10] = jnp.zeros((128, 256), f32)
 
     def forward(n):
@@ -214,15 +230,12 @@
             arrived(0, n)
             arrived(1, n)
             forward(n).start()
-            kt[n] = kv[n, :, 0:128].T
 
     @pl.loop(0, 8)
     def _(o):
         zs = (z + 8 - shift(o)) % 8
         for c in range(2):
-            n = zs * 2 + c
-            forward(n).wait_recv()
-            kt[16 + n] = kv[16 + n, :, 0:128].T
+            forward(zs * 2 + c).wait_recv()
 
     cols = pl.ds(pl.multiple_of((xb * 8 + z) * 128, 128), 128)
     row = xb * 8 + z
@@ -257,31 +270,41 @@
         for c in range(2):
             arrived(2, zs * 2 + c)
             arrived(3, zs * 2 + c)
-        for c, sp in ((0, sp0), (1, sp1)):
-            attend_block(zs * 2 + c, idx, qd, kv, kt, sp, x, dq)
+        a, b = zs * 2, zs * 2 + 1
+        scores(a, idx, qd, kv, sp0)
+        scores(b, idx, qd, kv, sp1)
+        softmax_grads(a, sp0, x)
+        query_grad(a, idx, kv, x, dq)
+        softmax_grads(b, sp1, x)
+        query_grad(b, idx, kv, x, dq)
         for c in range(2):
             send(0, zs * 2 + c, zs, c)
+        u = zs // 4
+        rows = [
+            jnp.concatenate([x[slot[a * TILES + t]], x[slot[b * TILES + t]]], axis=1)
+            for t in range(8, TILES)
+        ]
+        add = dot(jnp.concatenate(rows, axis=0), qd[pl.ds(a, 2)].reshape(512, 256))
+        for t in range(5):
+            near[u * 5 + t] += add[t * 128 : (t + 1) * 128]
+            part[u * 5 + t] += add[(t + 5) * 128 : (t + 6) * 128]
 
     def tile_sum(u, t):
         rows = jnp.concatenate([x[slot[(u * 8 + i) * TILES + t]] for i in range(8)], axis=1)
         return dot(rows, qd[pl.ds(u * 8, 8)].reshape(2048, 256))
 
-    @pl.loop(0, 10)
-    def _(t):
-        part[t] = tile_sum(t // 5, 13 + t % 5)
-
     swap = remote(part, recv.at[0:10], psem.at[0], psem.at[1], here_dev)
     swap.start()
 
-    @pl.loop(0, 10)
-    def _(t):
-        near[t] = tile_sum(t // 5, 8 + t % 5)
+    @pl.loop(0, 16)
+    def _(n):
+        own[n] = tile_sum(n // 8, n % 8)
 
     swap.wait()
 
     @pl.loop(0, 8)
     def _(o):
-        zs = (z + 8 - shift(o)) % 8
+        zs = (z + 8 - shift(7 - o)) % 8
         u = zs // 4
         for c in range(2):
             n = zs * 2 + c
@@ -289,7 +312,7 @@
             r = u * 5 + pool_place(
                 pool, (ctx // 4) * 4 + (1 - core) * 2 + u, 1, n % 8, 10 - u * 5
             )
-            fin[n] = (tile_sum(u, n % 8) + near[p] + recv[r]).astype(bf16)
+            fin[n] = (own[n] + near[p] + recv[r]).astype(bf16)
             send(1, n, zs, c)
             send(2, n, zs, c)
 
@@ -343,13 +366,13 @@
         scratch_shapes=[
             pltpu.VMEM((16, 256, 256), bf16),
             pltpu.VMEM((32, 128, 256), bf16),
-            pltpu.VMEM((32, 128, 128), bf16),
             pltpu.VMEM((ZERO + 1, 128, 256), bf16),
             pltpu.VMEM((NKEY * 128, 256), f32),
             pltpu.VMEM((NKEY * 128, 256), f32),
             pltpu.VMEM((16, 128, 128), bf16),
             pltpu.VMEM((10, 128, 256), f32),
             pltpu.VMEM((11, 128, 256), f32),
+            pltpu.VMEM((16, 128, 256), f32),
             pltpu.VMEM((11, 128, 256), f32),
             pltpu.VMEM((16, 128, 256), bf16),
             pltpu.VMEM((2, 4, 8), i32),

time: 107 us -> 103 us (0.963)
  the two profiles are of different devices: /device:TPU:81 before, /device:TPU:1 now
where the time goes in v3:
time: 103 us
  Pallas kernels  98.2 us (95%)
  local copies, waits for them, and re-layouts  3.97 us (4%)
    pallas_call x1, Pallas kernels, per_device(): pl.pallas_call(kernel, name='butterfly', out_shape=tuple((jax.ShapeDtypeS...  98.2 us
    unnamed x7, local copies, waits for them, and re-layouts  3.97 us

profile of v3, /device:TPU:1, one launch (start us, length us, event | category | flops | bytes accessed | tf_op | source)
XLA Modules:
  0.0 102.8 jit_solution(16614271024919795895)
XLA Ops:
  0.6 98.2 %butterfly.1 = (bf16[128,2048]{1,0:T(8,128)(2,1)}, bf16[128,2048]{1,0:T(8,128)(2,1)}, bf16[128,2048]{1,0:T(8,128)(2,1)}) custom-call(bf16[128,2048]{1,0:T(8,128)(2,1)} %q.1, bf16[128,2048]{1,0:T(8,128)(2,1)} %k.1, bf16[128,2048]{1,0:T(8,128)(2,1)} %v.1, bf16[128,2048]{1,0:T(8,128)(2,1)} %g.1, s32[4,8]{1,0:T(4,128)} %bitcast.5, s32[2,4,8]{2,1,0:T(4,128)} %bitcast.4, ...), custom_call_target="tpu_custom_call" | custom-call | tf_op jit(solution)/shard_map/butterfly/pallas_call | solution.py:360
  98.8 0.0 copy-start.1
  98.8 1.9 %copy.13 = bf16[128,2048]{1,0:T(8,128)(2,1)} copy(bf16[128,2048]{1,0:T(8,128)(2,1)} %get-tuple-element.6) | data formatting | bytes 1048576
  100.8 0.0 copy-done.1
  100.8 0.0 copy-start
  100.8 0.8 copy.14
  101.6 0.4 copy-done
  102.0 0.8 copy.15
Async XLA Ops:
  98.8 2.0 %copy-start.1 = (bf16[128,2048]{1,0:T(8,128)(2,1)S(1)}, bf16[128,2048]{1,0:T(8,128)(2,1)}, u32[]{:S(2)}) copy-start(bf16[128,2048]{1,0:T(8,128)(2,1)} %get-tuple-element.7) | copy-start | bytes 1572868
  100.8 1.2 %copy-start = (bf16[128,2048]{1,0:T(8,128)(2,1)S(1)}, bf16[128,2048]{1,0:T(8,128)(2,1)}, u32[]{:S(2)}) copy-start(bf16[128,2048]{1,0:T(8,128)(2,1)} %get-tuple-element.8) | copy-start | bytes 1572868

commit v4 on v3

--- a/solution.py
+++ b/solution.py
@@ -116,10 +116,10 @@
 
 
 def kernel(
-    q, k, v, g, offsets, partner_picks, pool,
+    q, k, v, g, offsets, partner_picks, all_pools,
     oq, ok, ov,
-    qd, kv, x, sp0, sp1, dq, part, near, own, recv, fin,
-    voffs, vpicks, offs, picks, idx, slot,
+    qd, kv, x, sp0, sp1, dq, part, near, own, part_half, recv, fin,
+    voffs, vpicks, offs, picks, pool, idx, slot,
     ssem, rsem, fsem, msem, lsem, osem, orsem, psem,
 ):
     ctx, xb, z, core = place()
@@ -142,6 +142,8 @@
             barrier, 1, device_id=device(ctx, core, z, xb), device_id_type=MESH
         )
 
+    pool_copy = pltpu.make_async_copy(all_pools, pool, lsem.at[2])
+    pool_copy.start()
     qd[:, 0:128, 128:256] = jnp.zeros((16, 128, 128), bf16)
     qd[:, 128:256, 0:128] = jnp.zeros((16, 128, 128), bf16)
     pl.semaphore_wait(barrier, 23 + away.astype(jnp.int32))
@@ -213,11 +215,12 @@
         local = pltpu.make_async_copy(src, dst, lsem.at[b])
         local.start()
         local.wait()
+    pool_copy.wait()
     tables(offs, picks, pool, group0, idx, slot)
     x[ZERO] = jnp.zeros((128, 256), bf16)
     near[...] = jnp.zeros((11, 128, 256), f32)
     part[...] = jnp.zeros((10, 128, 256), f32)
-    recv[10] = jnp.zeros((128, 256), f32)
+    recv[10] = jnp.zeros((128, 256), bf16)
 
     def forward(n):
         return remote(kv.at[n], kv.at[16 + n], fsem.at[0, n], fsem.at[1, n], here_dev)
@@ -264,12 +267,12 @@
         def _():
             pltpu.make_async_copy(result(a, n), outs[a].at[:, cols], orsem.at[a, row]).start()
 
-    @pl.loop(0, 8)
-    def _(o):
-        zs = (z + 8 - shift(o)) % 8
+    def await_pair(zs):
         for c in range(2):
             arrived(2, zs * 2 + c)
             arrived(3, zs * 2 + c)
+
+    def attend_pair(zs):
         a, b = zs * 2, zs * 2 + 1
         scores(a, idx, qd, kv, sp0)
         scores(b, idx, qd, kv, sp1)
@@ -277,8 +280,9 @@
         query_grad(a, idx, kv, x, dq)
         softmax_grads(b, sp1, x)
         query_grad(b, idx, kv, x, dq)
-        for c in range(2):
-            send(0, zs * 2 + c, zs, c)
+
+    def add_pair(zs):
+        a, b = zs * 2, zs * 2 + 1
         u = zs // 4
         rows = [
             jnp.concatenate([x[slot[a * TILES + t]], x[slot[b * TILES + t]]], axis=1)
@@ -289,32 +293,67 @@
             near[u * 5 + t] += add[t * 128 : (t + 1) * 128]
             part[u * 5 + t] += add[(t + 5) * 128 : (t + 6) * 128]
 
+    def source(o):
+        return (z + 8 - shift(o)) % 8
+
+    @pl.loop(0, 7)
+    def _(o):
+        zs = source(o)
+        await_pair(zs)
+        attend_pair(zs)
+        add_pair(zs)
+
+    await_pair(source(7))
+
+    @pl.loop(1, 8)
+    def _(o):
+        zs = source(7 - o)
+        for c in range(2):
+            send(0, zs * 2 + c, zs, c)
+
+    attend_pair(source(7))
+    for c in range(2):
+        send(0, source(7) * 2 + c, source(7), c)
+    add_pair(source(7))
+
     def tile_sum(u, t):
         rows = jnp.concatenate([x[slot[(u * 8 + i) * TILES + t]] for i in range(8)], axis=1)
         return dot(rows, qd[pl.ds(u * 8, 8)].reshape(2048, 256))
 
-    swap = remote(part, recv.at[0:10], psem.at[0], psem.at[1], here_dev)
+    part_half[...] = part[...].astype(bf16)
+    swap = remote(part_half, recv.at[0:10], psem.at[0], psem.at[1], here_dev)
     swap.start()
 
-    @pl.loop(0, 16)
-    def _(n):
-        own[n] = tile_sum(n // 8, n % 8)
+    def finish(n, zs, c, local):
+        u = zs // 4
+        p = (1 - u) * 5 + pool_place(pool, group0 + 1 - u, 0, n % 8, 10 - (1 - u) * 5)
+        r = u * 5 + pool_place(pool, (ctx // 4) * 4 + (1 - core) * 2 + u, 1, n % 8, 10 - u * 5)
+        fin[n] = (local + near[p] + recv[r].astype(f32)).astype(bf16)
+        send(1, n, zs, c)
+        send(2, n, zs, c)
+
+    @pl.loop(0, 4)
+    def _(o):
+        zs = source(7 - o)
+        for c in range(2):
+            n = zs * 2 + c
+            own[n] = tile_sum(zs // 4, n % 8)
 
     swap.wait()
 
-    @pl.loop(0, 8)
-    def _(o):
-        zs = (z + 8 - shift(7 - o)) % 8
-        u = zs // 4
+    @pl.loop(0, 4)
+    def _(o):
+        zs = source(7 - o)
         for c in range(2):
             n = zs * 2 + c
-            p = (1 - u) * 5 + pool_place(pool, group0 + 1 - u, 0, n % 8, 10 - (1 - u) * 5)
-            r = u * 5 + pool_place(
-                pool, (ctx // 4) * 4 + (1 - core) * 2 + u, 1, n % 8, 10 - u * 5
-            )
-            fin[n] = (own[n] + near[p] + recv[r]).astype(bf16)
-            send(1, n, zs, c)
-            send(2, n, zs, c)
+            finish(n, zs, c, own[n])
+
+    @pl.loop(4, 8)
+    def _(o):
+        zs = source(7 - o)
+        for c in range(2):
+            n = zs * 2 + c
+            finish(n, zs, c, tile_sum(zs // 4, n % 8))
 
     @pl.loop(0, 16)
     def _(r):
@@ -352,16 +391,34 @@
                     out_copy(a, n, zs, c).wait_send()
 
 
+PIECES = [(a, h) for h in range(2) for a in range(3)]
+
+
+def copy_kernel(a, b, c, oa, ob, oc, buf, sem):
+    srcs, dsts = (a, b, c), (oa, ob, oc)
+    ins, outs = [], []
+    for i, (r, h) in enumerate(PIECES):
+        rows = pl.ds(h * 64, 64)
+        ins.append(pltpu.make_async_copy(srcs[r].at[rows], buf.at[r, rows], sem.at[0, i]))
+        outs.append(pltpu.make_async_copy(buf.at[r, rows], dsts[r].at[rows], sem.at[1, i]))
+    for cp in ins:
+        cp.start()
+    for cp, out in zip(ins, outs):
+        cp.wait()
+        out.start()
+    for cp in outs:
+        cp.wait()
+
+
 def per_device(q, k, v, g, local_offsets, partner_pool, partner_picks):
     hbm = pl.BlockSpec(memory_space=pltpu.HBM)
-    sm = pl.BlockSpec(memory_space=pltpu.SMEM)
     dma = pltpu.SemaphoreType.DMA
     i32 = jnp.int32
-    return pl.pallas_call(
+    results = pl.pallas_call(
         kernel,
         name="butterfly",
         out_shape=tuple(jax.ShapeDtypeStruct((128, 2048), bf16) for _ in range(3)),
-        in_specs=[hbm] * 6 + [sm],
+        in_specs=[hbm] * 7,
         out_specs=(hbm, hbm, hbm),
         scratch_shapes=[
             pltpu.VMEM((16, 256, 256), bf16),
@@ -373,19 +430,21 @@
             pltpu.VMEM((10, 128, 256), f32),
             pltpu.VMEM((11, 128, 256), f32),
             pltpu.VMEM((16, 128, 256), f32),
-            pltpu.VMEM((11, 128, 256), f32),
+            pltpu.VMEM((10, 128, 256), bf16),
+            pltpu.VMEM((11, 128, 256), bf16),
             pltpu.VMEM((16, 128, 256), bf16),
             pltpu.VMEM((2, 4, 8), i32),
             pltpu.VMEM((2, 2, 4, 8), i32),
             pltpu.SMEM((2, 4, 8), i32),
             pltpu.SMEM((2, 2, 4, 8), i32),
+            pltpu.SMEM((5, 2, 32), i32),
             pltpu.SMEM((16 * NKEY,), i32),
             pltpu.SMEM((16 * TILES,), i32),
             dma((4, 16)),
             dma((4, 16)),
             dma((2, 16)),
             dma((2, 4)),
-            dma((2,)),
+            dma((3,)),
             dma((3, 16)),
             dma((3, 16)),
             dma((2,)),
@@ -394,6 +453,15 @@
             collective_id=0, has_side_effects=True, vmem_limit_bytes=58 << 20
         ),
     )(q, k, v, g, local_offsets.T, partner_picks.transpose(1, 2, 0), partner_pool.transpose(2, 1, 0))
+    return pl.pallas_call(
+        copy_kernel,
+        name="results",
+        out_shape=tuple(jax.ShapeDtypeStruct((128, 2048), bf16) for _ in range(3)),
+        in_specs=[hbm] * 3,
+        out_specs=(hbm, hbm, hbm),
+        scratch_shapes=[pltpu.VMEM((3, 128, 2048), bf16), dma((2, 6))],
+        compiler_params=pltpu.CompilerParams(vmem_limit_bytes=58 << 20),
+    )(*results)
 
 
 def solution(mesh):

time: 103 us -> 100 us (0.971)
  local copies, waits for them, and re-layouts: 3.97 us -> 0 us
    unnamed x7 -> x0, local copies, waits for them, and re-layouts: 3.97 us -> none
    pallas_call x0 -> x1, Pallas kernels: none -> 2.19 us  [per_device(): pl.pallas_call(copy_kernel, name='results', out_shape=tuple((jax.ShapeDty...]
    pallas_call x1, Pallas kernels: 98.2 us -> 97 us  [per_device(): pl.pallas_call(kernel, name='butterfly', out_shape=tuple((jax.ShapeDtypeS...]
where the time goes in v4:
time: 100 us; the launch traced here: 99.9 us
  Pallas kernels  99.2 us (99%)
    pallas_call x1, Pallas kernels, per_device(): pl.pallas_call(kernel, name='butterfly', out_shape=tuple((jax.ShapeDtypeS...  97 us
    pallas_call x1, Pallas kernels, per_device(): pl.pallas_call(copy_kernel, name='results', out_shape=tuple((jax.ShapeDty...  2.19 us

profile of v4, /device:TPU:1, one launch (start us, length us, event | category | flops | bytes accessed | tf_op | source)
XLA Modules:
  0.0 99.9 jit_solution(14182641230490117814)
XLA Ops:
  0.6 97.0 %butterfly.1 = (bf16[128,2048]{1,0:T(8,128)(2,1)}, bf16[128,2048]{1,0:T(8,128)(2,1)}, bf16[128,2048]{1,0:T(8,128)(2,1)}) custom-call(bf16[128,2048]{1,0:T(8,128)(2,1)} %q.1, bf16[128,2048]{1,0:T(8,128)(2,1)} %k.1, bf16[128,2048]{1,0:T(8,128)(2,1)} %v.1, bf16[128,2048]{1,0:T(8,128)(2,1)} %g.1, s32[4,8]{1,0:T(4,128)} %bitcast.5, s32[2,4,8]{2,1,0:T(4,128)} %bitcast.4, ...), custom_call_target="tpu_custom_call" | custom-call | tf_op jit(solution)/shard_map/butterfly/pallas_call | solution.py:417
  97.7 2.2 %results.1 = (bf16[128,2048]{1,0:T(8,128)(2,1)}, bf16[128,2048]{1,0:T(8,128)(2,1)}, bf16[128,2048]{1,0:T(8,128)(2,1)}) custom-call(bf16[128,2048]{1,0:T(8,128)(2,1)} %get-tuple-element.6.a, bf16[128,2048]{1,0:T(8,128)(2,1)} %get-tuple-element.7.b, bf16[128,2048]{1,0:T(8,128)(2,1)} %get-tuple-element.8.c), custom_call_target="tpu_custom_call" | custom-call | tf_op jit(solution)/shard_map/results/pallas_call | solution.py:456

commit v5 on v4

--- a/solution.py
+++ b/solution.py
@@ -296,25 +296,14 @@
     def source(o):
         return (z + 8 - shift(o)) % 8
 
-    @pl.loop(0, 7)
+    @pl.loop(0, 8)
     def _(o):
         zs = source(o)
         await_pair(zs)
         attend_pair(zs)
+        for c in range(2):
+            send(0, zs * 2 + c, zs, c)
         add_pair(zs)
-
-    await_pair(source(7))
-
-    @pl.loop(1, 8)
-    def _(o):
-        zs = source(7 - o)
-        for c in range(2):
-            send(0, zs * 2 + c, zs, c)
-
-    attend_pair(source(7))
-    for c in range(2):
-        send(0, source(7) * 2 + c, source(7), c)
-    add_pair(source(7))
 
     def tile_sum(u, t):
         rows = jnp.concatenate([x[slot[(u * 8 + i) * TILES + t]] for i in range(8)], axis=1)

time: 100 us -> 98.2 us (0.982)
  Pallas kernels: 99.2 us -> 97.4 us
    pallas_call x1, Pallas kernels: 97 us -> 95.2 us  [per_device(): pl.pallas_call(kernel, name='butterfly', out_shape=tuple((jax.ShapeDtypeS...]
where the time goes in v5:
time: 98.2 us; the launch traced here: 98 us
  Pallas kernels  97.4 us (99%)
    pallas_call x1, Pallas kernels, per_device(): pl.pallas_call(kernel, name='butterfly', out_shape=tuple((jax.ShapeDtypeS...  95.2 us
    pallas_call x1, Pallas kernels, per_device(): pl.pallas_call(copy_kernel, name='results', out_shape=tuple((jax.ShapeDty...  2.19 us

profile of v5, /device:TPU:1, one launch (start us, length us, event | category | flops | bytes accessed | tf_op | source)
XLA Modules:
  0.0 98.0 jit_solution(4703518855988249541)
XLA Ops:
  0.6 95.2 %butterfly.1 = (bf16[128,2048]{1,0:T(8,128)(2,1)}, bf16[128,2048]{1,0:T(8,128)(2,1)}, bf16[128,2048]{1,0:T(8,128)(2,1)}) custom-call(bf16[128,2048]{1,0:T(8,128)(2,1)} %q.1, bf16[128,2048]{1,0:T(8,128)(2,1)} %k.1, bf16[128,2048]{1,0:T(8,128)(2,1)} %v.1, bf16[128,2048]{1,0:T(8,128)(2,1)} %g.1, s32[4,8]{1,0:T(4,128)} %bitcast.5, s32[2,4,8]{2,1,0:T(4,128)} %bitcast.4, ...), custom_call_target="tpu_custom_call" | custom-call | tf_op jit(solution)/shard_map/butterfly/pallas_call | solution.py:406
  95.9 2.2 %results.1 = (bf16[128,2048]{1,0:T(8,128)(2,1)}, bf16[128,2048]{1,0:T(8,128)(2,1)}, bf16[128,2048]{1,0:T(8,128)(2,1)}) custom-call(bf16[128,2048]{1,0:T(8,128)(2,1)} %get-tuple-element.6.a, bf16[128,2048]{1,0:T(8,128)(2,1)} %get-tuple-element.7.b, bf16[128,2048]{1,0:T(8,128)(2,1)} %get-tuple-element.8.c), custom_call_target="tpu_custom_call" | custom-call | tf_op jit(solution)/shard_map/results/pallas_call | solution.py:445

commit v6 on v5

--- a/solution.py
+++ b/solution.py
@@ -293,6 +293,17 @@
             near[u * 5 + t] += add[t * 128 : (t + 1) * 128]
             part[u * 5 + t] += add[(t + 5) * 128 : (t + 6) * 128]
 
+    def swap_half(u):
+        rows = pl.ds(u * 5, 5)
+        return remote(
+            part_half.at[rows], recv.at[rows], psem.at[0, u], psem.at[1, u], here_dev
+        )
+
+    def start_swap(u):
+        rows = pl.ds(u * 5, 5)
+        part_half[rows] = part[rows].astype(bf16)
+        swap_half(u).start()
+
     def source(o):
         return (z + 8 - shift(o)) % 8
 
@@ -300,6 +311,11 @@
     def _(o):
         zs = source(o)
         await_pair(zs)
+
+        @pl.when(o == 7)
+        def _():
+            start_swap(1 - zs // 4)
+
         attend_pair(zs)
         for c in range(2):
             send(0, zs * 2 + c, zs, c)
@@ -309,9 +325,7 @@
         rows = jnp.concatenate([x[slot[(u * 8 + i) * TILES + t]] for i in range(8)], axis=1)
         return dot(rows, qd[pl.ds(u * 8, 8)].reshape(2048, 256))
 
-    part_half[...] = part[...].astype(bf16)
-    swap = remote(part_half, recv.at[0:10], psem.at[0], psem.at[1], here_dev)
-    swap.start()
+    start_swap(source(7) // 4)
 
     def finish(n, zs, c, local):
         u = zs // 4
@@ -321,23 +335,24 @@
         send(1, n, zs, c)
         send(2, n, zs, c)
 
-    @pl.loop(0, 4)
+    @pl.loop(0, 3)
     def _(o):
         zs = source(7 - o)
         for c in range(2):
             n = zs * 2 + c
             own[n] = tile_sum(zs // 4, n % 8)
 
-    swap.wait()
-
-    @pl.loop(0, 4)
+    swap_half(0).wait()
+    swap_half(1).wait()
+
+    @pl.loop(0, 3)
     def _(o):
         zs = source(7 - o)
         for c in range(2):
             n = zs * 2 + c
             finish(n, zs, c, own[n])
 
-    @pl.loop(4, 8)
+    @pl.loop(3, 8)
     def _(o):
         zs = source(7 - o)
         for c in range(2):
@@ -436,7 +451,7 @@
             dma((3,)),
             dma((3, 16)),
             dma((3, 16)),
-            dma((2,)),
+            dma((2, 2)),
         ],
         compiler_params=pltpu.CompilerParams(
             collective_id=0, has_side_effects=True, vmem_limit_bytes=58 << 20

time: 98.2 us -> 98.1 us (level)
  no operation moved by 1% of the time
where the time goes in v6:
time: 98.1 us; the launch traced here: 97.9 us
  Pallas kernels  97.3 us (99%)
    pallas_call x1, Pallas kernels, per_device(): pl.pallas_call(kernel, name='butterfly', out_shape=tuple((jax.ShapeDtypeS...  95.1 us
    pallas_call x1, Pallas kernels, per_device(): pl.pallas_call(copy_kernel, name='results', out_shape=tuple((jax.ShapeDty...  2.19 us

profile of v6, /device:TPU:1, one launch (start us, length us, event | category | flops | bytes accessed | tf_op | source)
XLA Modules:
  0.0 97.9 jit_solution(10782907888294218548)
XLA Ops:
  0.6 95.1 %butterfly.1 = (bf16[128,2048]{1,0:T(8,128)(2,1)}, bf16[128,2048]{1,0:T(8,128)(2,1)}, bf16[128,2048]{1,0:T(8,128)(2,1)}) custom-call(bf16[128,2048]{1,0:T(8,128)(2,1)} %q.1, bf16[128,2048]{1,0:T(8,128)(2,1)} %k.1, bf16[128,2048]{1,0:T(8,128)(2,1)} %v.1, bf16[128,2048]{1,0:T(8,128)(2,1)} %g.1, s32[4,8]{1,0:T(4,128)} %bitcast.5, s32[2,4,8]{2,1,0:T(4,128)} %bitcast.4, ...), custom_call_target="tpu_custom_call" | custom-call | tf_op jit(solution)/shard_map/butterfly/pallas_call | solution.py:421
  95.7 2.2 %results.1 = (bf16[128,2048]{1,0:T(8,128)(2,1)}, bf16[128,2048]{1,0:T(8,128)(2,1)}, bf16[128,2048]{1,0:T(8,128)(2,1)}) custom-call(bf16[128,2048]{1,0:T(8,128)(2,1)} %get-tuple-element.6.a, bf16[128,2048]{1,0:T(8,128)(2,1)} %get-tuple-element.7.b, bf16[128,2048]{1,0:T(8,128)(2,1)} %get-tuple-element.8.c), custom_call_target="tpu_custom_call" | custom-call | tf_op jit(solution)/shard_map/results/pallas_call | solution.py:460
